TPU v7x, 32 devices: a whole 2x2x4 slice. The times are simulated.
32 devices in a mesh: mx: 4 (over z), my: 8 (over y, x, core).
Axes of the slice: x: 2, y: 2, z: 4, core: 2. Of those that a mesh axis runs over, the one named last changes fastest.
Arguments:
- noise: bfloat16 [64, 131072], P(None, ('mx', 'my')), may hold values from -6 to 6
- blocks: bfloat16 [2048, 6, 64, 64], P(('mx', 'my')), may hold values from -0.21875 to 0.21875
- pattern: int32 [2048, 6], P(('mx', 'my')), may hold values from 0 to 127
- send_lists: int32 [128, 16], P(('mx', 'my')), may hold values from 0 to 63
- proj_weight: bfloat16 [2048, 2, 64, 128], P(('mx', 'my')), may hold values from -0.0625 to 0.0625
- tile_of: int32 [2048, 2], P(('mx', 'my')), may hold values from 0 to 31, all different within a row
Outputs:
- fields: bfloat16 [64, 131072], P(None, ('mx', 'my'))
- tile_values: float32 [32, 64, 128], P(('mx', 'my'))
Inputs may be any that keep to these rules, and one draw needn't show every extreme that they name: `tile_of`: each row names 2 different tiles, and every tile is named by some row.
All inputs are finite; a program needn't handle non-finite values.
Results may differ from a plain program's by a relative error of at most 0.0053.
Values may be sent and summed in bfloat16 or wider, within the bound.
No kernel may reach another device: no remote copies, remote signals or barrier semaphores. Data moves between devices by JAX's collectives and lax.ppermute only.
A program may use at most 128 MiB of HBM per device.

v0:
```python
import jax
import jax.numpy as jnp
from jax import lax
from jax.sharding import PartitionSpec as P

ITERS = 4
TILES_DEV = 1


COEFFICIENTS = (0.8, 0.6, -0.45, 0.35, -0.3)


def passed_along(block, axis, distance):
    devices = range(lax.axis_size(axis))
    route = [(i - distance, i) for i in devices if i - distance in devices]
    return lax.ppermute(block, axis, route)


def extend_blocks(rounded, send_lists):
    payload = [jnp.take(rounded, send_lists[which], axis=1) for which in range(4)]
    below = passed_along(payload[0], "mx", 1)
    above = passed_along(payload[1], "mx", -1)
    left = passed_along(payload[2], "my", 1)
    right = passed_along(payload[3], "my", -1)
    return jnp.concatenate([rounded, below, above, left, right], axis=1)


def operate(values, send_lists, pattern, blocks):
    rounded = values.astype(jnp.bfloat16)
    extended = extend_blocks(rounded, send_lists)
    columns = jnp.take(extended, pattern, axis=1)
    return jnp.einsum("fbkm,bkmn->fbn", columns, blocks, preferred_element_type=jnp.float32)


def shards(noise, blocks, pattern, send_lists, proj_weight, tile_of):
    fields_count = noise.shape[0]
    block_count = blocks.shape[0]
    node_width = blocks.shape[2]
    cell_count = proj_weight.shape[3]
    state = noise.astype(jnp.float32).reshape(fields_count, block_count, node_width)
    previous = state
    current = operate(state, send_lists, pattern, blocks)
    total = COEFFICIENTS[0] * previous + COEFFICIENTS[1] * current
    for degree in range(2, ITERS + 1):
        following = 2.0 * operate(current, send_lists, pattern, blocks) - previous
        total = total + COEFFICIENTS[degree] * following
        previous, current = (current, following)
    sample = total.astype(jnp.bfloat16)
    fields = sample.reshape(fields_count, block_count * node_width)
    contrib = jnp.einsum("fbm,bomc->bofc", sample, proj_weight, preferred_element_type=jnp.float32)
    flat = contrib.reshape(-1, fields_count * cell_count)
    tile_ids = tile_of.reshape(-1)
    start = jnp.int32(0)
    count = lax.axis_size("mx") * (TILES_DEV * lax.axis_size("my"))
    inside = (tile_ids >= start) & (tile_ids < start + count)
    local_ids = jnp.where(inside, tile_ids, count)
    summed = jax.ops.segment_sum(flat, local_ids, count + 1)[:count]
    row_group = lax.psum_scatter(
        summed.reshape(count, fields_count, cell_count), "mx", scatter_dimension=0, tiled=True
    )
    tile_values = lax.psum_scatter(row_group, "my", scatter_dimension=0, tiled=True)
    return (fields, tile_values)


def solution(mesh):
    in_specs = (
        P(None, ("mx", "my")),
        P(("mx", "my"), None, None, None),
        P(("mx", "my"), None),
        P(("mx", "my"), None),
        P(("mx", "my"), None, None, None),
        P(("mx", "my"), None),
    )
    out_specs = (P(None, ("mx", "my")), P(("mx", "my"), None, None))
    return jax.shard_map(shards, mesh=mesh, in_specs=in_specs, out_specs=out_specs, check_vma=False)
```

profile of v0, /device:TPU:0, one launch (start us, length us, event | category | flops | bytes accessed | tf_op | source)
XLA Modules:
  0.0 269.7 jit_solution(685685153310417820)
XLA Ops:
  7.2 2.9 %reshape.63 = bf16[64,64,64]{2,1,0:T(8,128)(2,1)} reshape(bf16[64,4096]{1,0:T(8,128)(2,1)} %param.10) | data formatting | bytes 1048576 | tf_op jit(solution)/shard_map/reshape | solution.py:40
  10.1 3.0 %fusion.46 = (bf16[64,64,64]{2,0,1:T(8,128)(2,1)S(1)}, bf16[64,128,64]{2,0,1:T(8,128)(2,1)}) fusion(bf16[64,64,64]{2,1,0:T(8,128)(2,1)} %reshape.63), kind=kLoop, calls=%fused_computation.123 | loop fusion | bytes 2097152 | tf_op jit(solution)/shard_map/reshape | solution.py:40
  14.6 5.7 %collective-permute-start = (bf16[64,16,64]{2,0,1:T(8,128)(2,1)}, bf16[64,16,64]{2,0,1:T(8,128)(2,1)}, u32[]{:S(2)}, u32[]{:S(2)}) collective-permute-start(bf16[64,16,64]{2,0,1:T(8,128)(2,1)} %select_bitcast_fusion.15), channel_id=1, source_target_pairs={{0,8},{8,16},{16,24},{1,9},{9,17},{17,25},{2,10},{10,18},{18,26},{... | collective-permute-start | bytes 393224 | tf_op jit(solution)/shard_map/ppermute | solution.py:16
  21.6 1.3 collective-permute-start.1
  24.4 2.2 collective-permute-start.2
  27.3 1.3 collective-permute-start.3
  29.2 1.7 constant_dynamic-update-slice_fusion.3
  31.6 1.7 constant_dynamic-update-slice_fusion.2
  33.3 1.7 constant_dynamic-update-slice_fusion.1
  35.7 5.6 %gather_fusion.4 = bf16[384,64,64]{2,1,0:T(8,128)(2,1)} fusion(bf16[64,128,64]{2,0,1:T(8,128)(2,1)} %constant_dynamic-update-slice_fusion, s32[1024]{0:T(1024)S(1)} %pad_clamp_fusion), kind=kCustom, calls=%fused_computation.1.clone | custom fusion | bytes 6292992 | tf_op jit(solution)/shard_map/jit(_take)/gather | solution.py:31
  41.3 6.8 %fusion.6 = f32[64,64,64,1]{2,1,3,0:T(8,128)S(1)} fusion(bf16[64,6,64,64]{3,2,1,0:T(8,128)(2,1)} %param.11, bf16[64,6,64,64]{3,2,1,0:T(8,128)(2,1)} %bitcast.143, pred[64,6]{1,0:T(8,128)(4,1)S(1)} %copy.26), kind=kOutput, calls=%fused_computation.27 | convolution fusion | flops 202899456 | bytes 7340416 | tf_op jit(solution)/shard_map/fbkm,bkmn->fbn/dot_general | solution.py:32
  48.2 1.6 constant_dynamic-update-slice_fusion.9
  49.9 1.3 gather_fusion.5
  52.4 1.3 gather_fusion.7
  55.4 3.7 %collective-permute-start.4 = (bf16[64,16,64]{2,0,1:T(8,128)(2,1)S(1)}, bf16[64,16,64]{2,0,1:T(8,128)(2,1)S(1)}, u32[]{:S(2)}, u32[]{:S(2)}) collective-permute-start(bf16[64,16,64]{2,0,1:T(8,128)(2,1)S(1)} %select_bitcast_fusion.11), channel_id=1, source_target_pairs={{0,8},{8,16},{16,24},{1,9},{9,17},{17,25},{2,10},{10,18},{18,26},{... | collective-permute-start | bytes 393224 | tf_op jit(solution)/shard_map/ppermute | solution.py:16
  60.1 1.3 collective-permute-start.5
  62.5 3.8 %collective-permute-start.6 = (bf16[64,16,64]{2,0,1:T(8,128)(2,1)S(1)}, bf16[64,16,64]{2,0,1:T(8,128)(2,1)S(1)}, u32[]{:S(2)}, u32[]{:S(2)}) collective-permute-start(bf16[64,16,64]{2,0,1:T(8,128)(2,1)S(1)} %select_bitcast_fusion.9), channel_id=1, source_target_pairs={{0,1},{1,2},{2,3},{3,4},{4,5},{5,6},{6,7},{8,9},{9,10},{10,11},{11... | collective-permute-start | bytes 393224 | tf_op jit(solution)/shard_map/ppermute | solution.py:16
  66.4 1.3 collective-permute-start.7
  68.4 1.8 collective-permute-done.5
  72.4 5.7 %gather_fusion.9 = bf16[384,64,64]{2,1,0:T(8,128)(2,1)} fusion(bf16[64,128,64]{2,0,1:T(8,128)(2,1)} %constant_dynamic-update-slice_fusion.5, s32[1024]{0:T(1024)S(1)} %pad_clamp_fusion), kind=kCustom, calls=%fused_computation.17.clone | custom fusion | bytes 6292992 | tf_op jit(solution)/shard_map/jit(_take)/gather | solution.py:31
  78.1 9.9 %constant_dynamic-update-slice_fusion.14 = (bf16[64,128,64]{2,0,1:T(8,128)(2,1)}, bf16[64,64,64]{2,0,1:T(8,128)(2,1)}, f32[64,64,64,1]{2,1,3,0:T(8,128)}) fusion(bf16[64,64,64]{2,1,0:T(8,128)(2,1)S(1)} %copy-done.1, bf16[64,6,64,64]{3,2,1,0:T(8,128)(2,1)} %param.11, bf16[64,6,64,64]{3,2,1,0:T(8,128)(2,1)} %bitcast.142, pred[64,6]{1,0:T(8,128)(4,1)S(1)} %copy.26), kind=kOutput, calls=%fused_computation.96 | convolution fusion | flops 203948032 | bytes 11010432 | tf_op jit(solution)/shard_map/fbkm,bkmn->fbn/dot_general | solution.py:32
  88.1 2.5 gather_fusion.10
  90.6 2.5 gather_fusion.11
  93.1 2.5 gather_fusion.12
  95.6 1.8 gather_fusion.13
  98.4 4.1 %collective-permute-start.8 = (bf16[64,16,64]{2,0,1:T(8,128)(2,1)S(1)}, bf16[64,16,64]{2,0,1:T(8,128)(2,1)S(1)}, u32[]{:S(2)}, u32[]{:S(2)}) collective-permute-start(bf16[64,16,64]{2,0,1:T(8,128)(2,1)S(1)} %select_bitcast_fusion.7), channel_id=1, source_target_pairs={{0,8},{8,16},{16,24},{1,9},{9,17},{17,25},{2,10},{10,18},{18,26},{... | collective-permute-start | bytes 393224 | tf_op jit(solution)/shard_map/ppermute | solution.py:16
  103.6 1.3 collective-permute-start.9
  106.0 7.3 %collective-permute-start.10 = (bf16[64,16,64]{2,0,1:T(8,128)(2,1)S(1)}, bf16[64,16,64]{2,0,1:T(8,128)(2,1)S(1)}, u32[]{:S(2)}, u32[]{:S(2)}) collective-permute-start(bf16[64,16,64]{2,0,1:T(8,128)(2,1)S(1)} %select_bitcast_fusion.5), channel_id=1, source_target_pairs={{0,1},{1,2},{2,3},{3,4},{4,5},{5,6},{6,7},{8,9},{9,10},{10,11},{11... | collective-permute-start | bytes 393224 | tf_op jit(solution)/shard_map/ppermute | solution.py:16
  113.3 1.3 collective-permute-start.11
  117.6 5.6 %gather_fusion.14 = bf16[384,64,64]{2,1,0:T(8,128)(2,1)} fusion(bf16[64,128,64]{2,0,1:T(8,128)(2,1)} %constant_dynamic-update-slice_fusion.10, s32[1024]{0:T(1024)S(1)} %pad_clamp_fusion), kind=kCustom, calls=%fused_computation.18.clone | custom fusion | bytes 6292992 | tf_op jit(solution)/shard_map/jit(_take)/gather | solution.py:31
  123.2 7.5 %fusion.29 = f32[64,64,64]{2,1,0:T(8,128)S(1)} fusion(f32[64,64,64,1]{2,1,3,0:T(8,128)} %copy-done.4, bf16[64,6,64,64]{3,2,1,0:T(8,128)(2,1)} %param.11, bf16[64,6,64,64]{3,2,1,0:T(8,128)(2,1)} %bitcast.144, pred[64,6]{1,0:T(8,128)(4,1)S(1)} %copy.26), kind=kOutput, calls=%fused_computation.55 | convolution fusion | flops 203423744 | bytes 8388992 | tf_op jit(solution)/shard_map/fbkm,bkmn->fbn/dot_general | solution.py:32
  130.6 2.2 constant_dynamic-update-slice_fusion.19
  132.8 2.5 gather_fusion.15
  135.3 2.5 gather_fusion.16
  137.8 2.5 gather_fusion.17
  140.3 1.8 gather_fusion.18
  143.2 4.3 %collective-permute-start.12 = (bf16[64,16,64]{2,0,1:T(8,128)(2,1)S(1)}, bf16[64,16,64]{2,0,1:T(8,128)(2,1)S(1)}, u32[]{:S(2)}, u32[]{:S(2)}) collective-permute-start(bf16[64,16,64]{2,0,1:T(8,128)(2,1)S(1)} %select_bitcast_fusion.3), channel_id=1, source_target_pairs={{0,8},{8,16},{16,24},{1,9},{9,17},{17,25},{2,10},{10,18},{18,26},{... | collective-permute-start | bytes 393224 | tf_op jit(solution)/shard_map/ppermute | solution.py:16
  148.6 1.3 collective-permute-start.13
  150.9 7.1 %collective-permute-start.14 = (bf16[64,16,64]{2,0,1:T(8,128)(2,1)S(1)}, bf16[64,16,64]{2,0,1:T(8,128)(2,1)S(1)}, u32[]{:S(2)}, u32[]{:S(2)}) collective-permute-start(bf16[64,16,64]{2,0,1:T(8,128)(2,1)S(1)} %select_bitcast_fusion.1), channel_id=1, source_target_pairs={{0,1},{1,2},{2,3},{3,4},{4,5},{5,6},{6,7},{8,9},{9,10},{10,11},{11... | collective-permute-start | bytes 393224 | tf_op jit(solution)/shard_map/ppermute | solution.py:16
  158.1 1.3 collective-permute-start.15
  162.4 5.6 %gather_fusion.19 = bf16[384,64,64]{2,1,0:T(8,128)(2,1)} fusion(bf16[64,128,64]{2,0,1:T(8,128)(2,1)} %constant_dynamic-update-slice_fusion.15, s32[1024]{0:T(1024)S(1)} %pad_clamp_fusion), kind=kCustom, calls=%fused_computation.19.clone | custom fusion | bytes 6292992 | tf_op jit(solution)/shard_map/jit(_take)/gather | solution.py:31
  168.0 10.5 %fusion.27 = bf16[64,64,64]{2,0,1:T(8,128)(2,1)S(1)} fusion(f32[64,64,64,1]{2,1,3,0:T(8,128)} %copy-done.4, f32[64,64,64]{2,1,0:T(8,128)} %copy-done.5, f32[64,64,64,1]{2,1,3,0:T(8,128)} %get-tuple-element.26, bf16[64,6,64,64]{3,2,1,0:T(8,128)(2,1)} %param.11, bf16[64,6,64,64]{3,2,1,0:T(8,128)(2,1)} %bitcast.141, pred[64,6]{1,0:T(8,128)(4,1)S(1)} %copy.26, ...), kind=kOutput, calls=%fused_computation.50 | convolution fusion | flops 206831616 | bytes 10486144 | tf_op jit(solution)/shard_map/fbkm,bkmn->fbn/dot_general | solution.py:32
  178.5 2.6 fusion.36
  181.1 10.0 %scatter_custom_fusion = f32[33,8192]{1,0:T(8,128)S(1)} fusion(s32[128]{0:T(128)S(1)} %fusion.39, f32[16,8,64,128]{3,2,1,0:T(8,128)} %bitcast.140, f32[]{:T(128)} %constant.4.clone.1), kind=kCustom, calls=%fused_computation.37 | custom fusion | flops 1048576 | bytes 5275652 | tf_op jit(solution)/shard_map/scatter-add | solution.py:57
  192.5 34.5 %reduce-scatter.3.cloned.1.call-done = f32[8,64,128]{2,1,0:T(8,128)} async-done(((f32[32,64,128]{2,1,0:T(8,128)}), f32[8,64,128]{2,1,0:T(8,128)}) %reduce-scatter.3.cloned.1.call-update) | async-done | bytes 262160 | tf_op jit(solution)/shard_map/reduce_scatter | solution.py:58
  227.1 1.7 copy.39
  228.8 2.7 %reshape.65 = bf16[64,4096]{1,0:T(8,128)(2,1)} reshape(bf16[64,64,64]{2,1,0:T(8,128)(2,1)} %copy.39) | data formatting | bytes 1048576 | tf_op jit(solution)/shard_map/reshape | solution.py:49
  231.5 31.4 %reduce-scatter.5.cloned.1.call-done = f32[1,64,128]{2,1,0:T(8,128)} async-done(((f32[8,64,128]{2,1,0:T(8,128)}), f32[1,64,128]{2,1,0:T(8,128)}) %reduce-scatter.5.cloned.1.call-update) | async-done | bytes 32784 | tf_op jit(solution)/shard_map/reduce_scatter | solution.py:61
  (88 shorter events, 28.8 us)
Async XLA Ops:
  7.2 171.3 %copy-start = (bf16[64,2,64,128]{3,2,1,0:T(8,128)(2,1)S(1)}, bf16[64,2,64,128]{3,2,1,0:T(8,128)(2,1)}, u32[]{:S(2)}) copy-start(bf16[64,2,64,128]{3,2,1,0:T(8,128)(2,1)} %param.14) | copy-start | bytes 6291460
  7.2 6.0 %copy-start.7 = (s32[4,16]{1,0:T(4,128)S(1)}, s32[4,16]{1,0:T(4,128)}, u32[]{:S(2)}) copy-start(s32[4,16]{1,0:T(4,128)} %param.13) | copy-start | bytes 772
  7.2 219.8 %reduce-scatter.3.cloned.1.call-start = ((), (), s32[]{:S(2)}) async-start(), calls=%async_computation.2 | async-start | bytes 1310720 | tf_op jit(solution)/shard_map/reduce_scatter | solution.py:58
  13.2 15.4 %copy-start.6 = (s32[64,6]{0,1:T(8,128)S(1)}, s32[64,6]{0,1:T(8,128)}, u32[]{:S(2)}) copy-start(s32[64,6]{0,1:T(8,128)} %param.12) | copy-start | bytes 4612
  13.2 15.4 %copy-start.8 = (s32[64,2]{0,1:T(2,128)S(1)}, s32[64,2]{0,1:T(2,128)}, u32[]{:S(2)}) copy-start(s32[64,2]{0,1:T(2,128)} %param.15) | copy-start | bytes 1540
  14.6 14.6 %collective-permute-start = (bf16[64,16,64]{2,0,1:T(8,128)(2,1)}, bf16[64,16,64]{2,0,1:T(8,128)(2,1)}, u32[]{:S(2)}, u32[]{:S(2)}) collective-permute-start(bf16[64,16,64]{2,0,1:T(8,128)(2,1)} %select_bitcast_fusion.15), channel_id=1, source_target_pairs={{0,8},{8,16},{16,24},{1,9},{9,17},{17,25},{2,10},{10,18},{18,26},{... | collective-permute-start | bytes 393224 | tf_op jit(solution)/shard_map/ppermute | solution.py:16
  21.6 10.0 %collective-permute-start.1 = (bf16[64,16,64]{2,0,1:T(8,128)(2,1)}, bf16[64,16,64]{2,0,1:T(8,128)(2,1)}, u32[]{:S(2)}, u32[]{:S(2)}) collective-permute-start(bf16[64,16,64]{2,0,1:T(8,128)(2,1)} %select_bitcast_fusion.14), channel_id=1, source_target_pairs={{8,0},{16,8},{24,16},{9,1},{17,9},{25,17},{10,2},{18,10},{26,18},{... | collective-permute-start | bytes 393224 | tf_op jit(solution)/shard_map/ppermute | solution.py:16
  24.4 8.9 %collective-permute-start.2 = (bf16[64,16,64]{2,0,1:T(8,128)(2,1)}, bf16[64,16,64]{2,0,1:T(8,128)(2,1)}, u32[]{:S(2)}, u32[]{:S(2)}) collective-permute-start(bf16[64,16,64]{2,0,1:T(8,128)(2,1)} %select_bitcast_fusion.13), channel_id=1, source_target_pairs={{0,1},{1,2},{2,3},{3,4},{4,5},{5,6},{6,7},{8,9},{9,10},{10,11},{11... | collective-permute-start | bytes 393224 | tf_op jit(solution)/shard_map/ppermute | solution.py:16
  27.3 7.7 %collective-permute-start.3 = (bf16[64,16,64]{2,0,1:T(8,128)(2,1)S(1)}, bf16[64,16,64]{2,0,1:T(8,128)(2,1)S(1)}, u32[]{:S(2)}, u32[]{:S(2)}) collective-permute-start(bf16[64,16,64]{2,0,1:T(8,128)(2,1)S(1)} %select_bitcast_fusion.12), channel_id=1, source_target_pairs={{1,0},{2,1},{3,2},{4,3},{5,4},{6,5},{7,6},{9,8},{10,9},{11,10},{12... | collective-permute-start | bytes 393224 | tf_op jit(solution)/shard_map/ppermute | solution.py:16
  48.1 1.7 copy-start.4
  55.4 12.3 %collective-permute-start.4 = (bf16[64,16,64]{2,0,1:T(8,128)(2,1)S(1)}, bf16[64,16,64]{2,0,1:T(8,128)(2,1)S(1)}, u32[]{:S(2)}, u32[]{:S(2)}) collective-permute-start(bf16[64,16,64]{2,0,1:T(8,128)(2,1)S(1)} %select_bitcast_fusion.11), channel_id=1, source_target_pairs={{0,8},{8,16},{16,24},{1,9},{9,17},{17,25},{2,10},{10,18},{18,26},{... | collective-permute-start | bytes 393224 | tf_op jit(solution)/shard_map/ppermute | solution.py:16
  60.1 10.1 %collective-permute-start.5 = (bf16[64,16,64]{2,0,1:T(8,128)(2,1)S(1)}, bf16[64,16,64]{2,0,1:T(8,128)(2,1)S(1)}, u32[]{:S(2)}, u32[]{:S(2)}) collective-permute-start(bf16[64,16,64]{2,0,1:T(8,128)(2,1)S(1)} %select_bitcast_fusion.10), channel_id=1, source_target_pairs={{8,0},{16,8},{24,16},{9,1},{17,9},{25,17},{10,2},{18,10},{26,18},{... | collective-permute-start | bytes 393224 | tf_op jit(solution)/shard_map/ppermute | solution.py:16
  62.5 8.5 %collective-permute-start.6 = (bf16[64,16,64]{2,0,1:T(8,128)(2,1)S(1)}, bf16[64,16,64]{2,0,1:T(8,128)(2,1)S(1)}, u32[]{:S(2)}, u32[]{:S(2)}) collective-permute-start(bf16[64,16,64]{2,0,1:T(8,128)(2,1)S(1)} %select_bitcast_fusion.9), channel_id=1, source_target_pairs={{0,1},{1,2},{2,3},{3,4},{4,5},{5,6},{6,7},{8,9},{9,10},{10,11},{11... | collective-permute-start | bytes 393224 | tf_op jit(solution)/shard_map/ppermute | solution.py:16
  66.4 5.3 %collective-permute-start.7 = (bf16[64,16,64]{2,0,1:T(8,128)(2,1)S(1)}, bf16[64,16,64]{2,0,1:T(8,128)(2,1)S(1)}, u32[]{:S(2)}, u32[]{:S(2)}) collective-permute-start(bf16[64,16,64]{2,0,1:T(8,128)(2,1)S(1)} %select_bitcast_fusion.8), channel_id=1, source_target_pairs={{1,0},{2,1},{3,2},{4,3},{5,4},{6,5},{7,6},{9,8},{10,9},{11,10},{12... | collective-permute-start | bytes 393224 | tf_op jit(solution)/shard_map/ppermute | solution.py:16
  72.4 5.7 %copy-start.1 = (bf16[64,64,64]{2,1,0:T(8,128)(2,1)S(1)}, bf16[64,64,64]{2,1,0:T(8,128)(2,1)}, u32[]{:S(2)}) copy-start(bf16[64,64,64]{2,1,0:T(8,128)(2,1)} %reshape.63) | copy-start | bytes 1572868
  98.4 16.2 %collective-permute-start.8 = (bf16[64,16,64]{2,0,1:T(8,128)(2,1)S(1)}, bf16[64,16,64]{2,0,1:T(8,128)(2,1)S(1)}, u32[]{:S(2)}, u32[]{:S(2)}) collective-permute-start(bf16[64,16,64]{2,0,1:T(8,128)(2,1)S(1)} %select_bitcast_fusion.7), channel_id=1, source_target_pairs={{0,8},{8,16},{16,24},{1,9},{9,17},{17,25},{2,10},{10,18},{18,26},{... | collective-permute-start | bytes 393224 | tf_op jit(solution)/shard_map/ppermute | solution.py:16
  103.6 11.8 %collective-permute-start.9 = (bf16[64,16,64]{2,0,1:T(8,128)(2,1)S(1)}, bf16[64,16,64]{2,0,1:T(8,128)(2,1)S(1)}, u32[]{:S(2)}, u32[]{:S(2)}) collective-permute-start(bf16[64,16,64]{2,0,1:T(8,128)(2,1)S(1)} %select_bitcast_fusion.6), channel_id=1, source_target_pairs={{8,0},{16,8},{24,16},{9,1},{17,9},{25,17},{10,2},{18,10},{26,18},{... | collective-permute-start | bytes 393224 | tf_op jit(solution)/shard_map/ppermute | solution.py:16
  106.0 10.1 %collective-permute-start.10 = (bf16[64,16,64]{2,0,1:T(8,128)(2,1)S(1)}, bf16[64,16,64]{2,0,1:T(8,128)(2,1)S(1)}, u32[]{:S(2)}, u32[]{:S(2)}) collective-permute-start(bf16[64,16,64]{2,0,1:T(8,128)(2,1)S(1)} %select_bitcast_fusion.5), channel_id=1, source_target_pairs={{0,1},{1,2},{2,3},{3,4},{4,5},{5,6},{6,7},{8,9},{9,10},{10,11},{11... | collective-permute-start | bytes 393224 | tf_op jit(solution)/shard_map/ppermute | solution.py:16
  113.3 3.5 %collective-permute-start.11 = (bf16[64,16,64]{2,0,1:T(8,128)(2,1)S(1)}, bf16[64,16,64]{2,0,1:T(8,128)(2,1)S(1)}, u32[]{:S(2)}, u32[]{:S(2)}) collective-permute-start(bf16[64,16,64]{2,0,1:T(8,128)(2,1)S(1)} %select_bitcast_fusion.4), channel_id=1, source_target_pairs={{1,0},{2,1},{3,2},{4,3},{5,4},{6,5},{7,6},{9,8},{10,9},{11,10},{12... | collective-permute-start | bytes 393224 | tf_op jit(solution)/shard_map/ppermute | solution.py:16
  130.6 2.2 copy-start.5
  143.2 16.2 %collective-permute-start.12 = (bf16[64,16,64]{2,0,1:T(8,128)(2,1)S(1)}, bf16[64,16,64]{2,0,1:T(8,128)(2,1)S(1)}, u32[]{:S(2)}, u32[]{:S(2)}) collective-permute-start(bf16[64,16,64]{2,0,1:T(8,128)(2,1)S(1)} %select_bitcast_fusion.3), channel_id=1, source_target_pairs={{0,8},{8,16},{16,24},{1,9},{9,17},{17,25},{2,10},{10,18},{18,26},{... | collective-permute-start | bytes 393224 | tf_op jit(solution)/shard_map/ppermute | solution.py:16
  148.6 11.6 %collective-permute-start.13 = (bf16[64,16,64]{2,0,1:T(8,128)(2,1)S(1)}, bf16[64,16,64]{2,0,1:T(8,128)(2,1)S(1)}, u32[]{:S(2)}, u32[]{:S(2)}) collective-permute-start(bf16[64,16,64]{2,0,1:T(8,128)(2,1)S(1)} %select_bitcast_fusion.2), channel_id=1, source_target_pairs={{8,0},{16,8},{24,16},{9,1},{17,9},{25,17},{10,2},{18,10},{26,18},{... | collective-permute-start | bytes 393224 | tf_op jit(solution)/shard_map/ppermute | solution.py:16
  150.9 10.0 %collective-permute-start.14 = (bf16[64,16,64]{2,0,1:T(8,128)(2,1)S(1)}, bf16[64,16,64]{2,0,1:T(8,128)(2,1)S(1)}, u32[]{:S(2)}, u32[]{:S(2)}) collective-permute-start(bf16[64,16,64]{2,0,1:T(8,128)(2,1)S(1)} %select_bitcast_fusion.1), channel_id=1, source_target_pairs={{0,1},{1,2},{2,3},{3,4},{4,5},{5,6},{6,7},{8,9},{9,10},{10,11},{11... | collective-permute-start | bytes 393224 | tf_op jit(solution)/shard_map/ppermute | solution.py:16
  158.1 3.5 %collective-permute-start.15 = (bf16[64,16,64]{2,0,1:T(8,128)(2,1)S(1)}, bf16[64,16,64]{2,0,1:T(8,128)(2,1)S(1)}, u32[]{:S(2)}, u32[]{:S(2)}) collective-permute-start(bf16[64,16,64]{2,0,1:T(8,128)(2,1)S(1)} %select_bitcast_fusion), channel_id=1, source_target_pairs={{1,0},{2,1},{3,2},{4,3},{5,4},{6,5},{7,6},{9,8},{10,9},{11,10},{12... | collective-permute-start | bytes 393224 | tf_op jit(solution)/shard_map/ppermute | solution.py:16
  178.5 2.7 copy-start.2
  191.2 35.8 %copy-start.3 = (bf16[64,64,64]{2,0,1:T(8,128)(2,1)S(1)}, bf16[64,64,64]{2,0,1:T(8,128)(2,1)}, u32[]{:S(2)}) copy-start(bf16[64,64,64]{2,0,1:T(8,128)(2,1)} %copy-done.2) | copy-start | bytes 1572868
  192.4 70.4 %reduce-scatter.5.cloned.1.call-start = ((), (), s32[]{:S(2)}) async-start(), calls=%async_computation.3 | async-start | bytes 294912 | tf_op jit(solution)/shard_map/reduce_scatter | solution.py:61
Sparse Core Ops, SparseCore 0:
  192.6 34.4 reduce-scatter.2
  230.6 32.1 reduce-scatter.4
where the time goes:
time: 271 us; the launch traced here: 270 us
  local copies, waits for them, and re-layouts  74.8 us (28%)
  waiting for transfers between devices  68.5 us (25%)
  starting transfers between devices  48.5 us (18%)
  matrix products  37.3 us (14%)
  other arithmetic  26 us (10%)
  between operations  14.5 us (5%)
    ppermute x16, starting transfers between devices, passed_along(): return lax.ppermute(block, axis, route)  48.5 us
    dot_general x4, matrix products, operate(): jnp.einsum('fbkm,bkmn->fbn', columns, blocks, preferred_element_type=jnp....  34.6 us
    reduce_scatter x1, waiting for transfers between devices, shards(): lax.psum_scatter(summed.reshape(count, fields_count, cell_count), 'mx', s...  34.5 us
    reduce_scatter x1, waiting for transfers between devices, shards(): lax.psum_scatter(row_group, 'my', scatter_dimension=0, tiled=True)  31.4 us
    gather x16, local copies, waits for them, and re-layouts, extend_blocks(): jnp.take(rounded, send_lists[which], axis=1)  25.5 us
    gather x4, local copies, waits for them, and re-layouts, operate(): columns = jnp.take(extended, pattern, axis=1)  22.5 us
    unnamed x33, local copies, waits for them, and re-layouts  13.1 us
    select_n x16, other arithmetic, extend_blocks(): jnp.take(rounded, send_lists[which], axis=1)  12.1 us
  transfers between devices with their start and end apart: 18, of which 4 were waited for; matrix products, arithmetic and copies ran while one was open for 10% of the time, Pallas kernels for 0%

commit v1 on v0

v1 whole, which is shorter than its diff:
```python
import functools

import jax
import jax.numpy as jnp
from jax import lax
from jax.experimental import pallas as pl
from jax.experimental.pallas import tpu as pltpu
from jax.sharding import PartitionSpec as P

ITERS = 4
COEFFICIENTS = (0.8, 0.6, -0.45, 0.35, -0.3)
VMEM = pl.BlockSpec(memory_space=pltpu.VMEM)
SMEM = pl.BlockSpec(memory_space=pltpu.SMEM)
PARAMS = pltpu.CompilerParams(vmem_limit_bytes=24 << 20)
BF16 = jnp.bfloat16
F32 = jnp.float32


def lower_half(shape, width):
    return lax.broadcasted_iota(jnp.int32, shape, len(shape) - 1) < width


def both_halves(pair, width):
    first, second = pair[:, :width], pair[:, width:]
    return jnp.concatenate([first, first], 1), jnp.concatenate([second, second], 1)


def side_by_side(doubled, one, two, width):
    a, b = doubled[one], doubled[two]
    return jnp.where(lower_half(a.shape, width), a, b)


def fill_payloads(where_ref, sends_ref, doubled, payloads, width):
    for slot, payload in enumerate(payloads):
        row = where_ref[slot]
        for q in range(payload.shape[0]):
            payload[q] = side_by_side(doubled, sends_ref[row, 2 * q], sends_ref[row, 2 * q + 1], width)


def first_kernel(where_ref, sends_ref, noise_ref, doubled, *payloads):
    fields, nodes = noise_ref.shape
    lanes = doubled.shape[2]
    width = lanes // 2
    for q in range(nodes // lanes):
        doubled[2 * q], doubled[2 * q + 1] = both_halves(noise_ref[:, q * lanes : (q + 1) * lanes], width)
    fill_payloads(where_ref, sends_ref, doubled, payloads, width)


def weights_kernel(blocks_ref, out_ref):
    step = pl.program_id(0)
    pairs = blocks_ref.shape[0] // 2
    depth, width = blocks_ref.shape[1:]
    zero = jnp.zeros((depth, width), BF16)
    for r in range(pairs):
        out_ref[step * pairs + r, :depth] = jnp.concatenate([blocks_ref[2 * r], zero], 1)
        out_ref[step * pairs + r, depth:] = jnp.concatenate([zero, blocks_ref[2 * r + 1]], 1)


def unpack_halos(where_ref, halos, doubled, base, width):
    for slot, halo in enumerate(halos):
        count = 2 * halo.shape[0]
        start = base + where_ref[4 + slot] * count
        for q in range(halo.shape[0]):
            doubled[start + 2 * q], doubled[start + 2 * q + 1] = both_halves(halo[q], width)


def applied(pattern_ref, doubled, weights_ref, q, width):
    entries = pattern_ref.shape[0]
    wanted = [pattern_ref[k, 2 * q + side] for side in range(2) for k in range(entries)]
    columns = [side_by_side(doubled, wanted[k], wanted[k + 1], width) for k in range(0, 2 * entries, 2)]
    return jnp.dot(jnp.concatenate(columns, 1), weights_ref[q], preferred_element_type=F32)


def step_kernel(degree, where_ref, sends_ref, pattern_ref, weights_ref, halo_a, halo_b, halo_c, halo_d, *rest):
    if degree == 1:
        noise_ref, _, doubled, current_ref, total_ref, following, *payloads = rest
    else:
        previous_ref, total_in, _, doubled, current_ref, total_ref, following, *payloads = rest
    width = doubled.shape[2] // 2
    lanes = 2 * width
    blocks = pattern_ref.shape[1]
    unpack_halos(where_ref, (halo_a, halo_b, halo_c, halo_d), doubled, blocks, width)

    def body(q, carry):
        product = applied(pattern_ref, doubled, weights_ref, q, width)
        if degree == 1:
            start = noise_ref[:, pl.ds(pl.multiple_of(q * lanes, lanes), lanes)].astype(F32)
            value = product
            total_ref[q] = COEFFICIENTS[0] * start + COEFFICIENTS[1] * value
        else:
            if degree == 2:
                start = previous_ref[:, pl.ds(pl.multiple_of(q * lanes, lanes), lanes)].astype(F32)
            else:
                start = previous_ref[q]
            value = 2.0 * product - start
            total_ref[q] = total_in[q] + COEFFICIENTS[degree] * value
        current_ref[q] = value
        following[2 * q], following[2 * q + 1] = both_halves(value.astype(BF16), width)
        return carry

    lax.fori_loop(0, blocks // 2, body, 0, unroll=4)
    fill_payloads(where_ref, sends_ref, following, payloads, width)


def last_kernel(
    where_ref, pattern_ref, slots_ref, weights_ref, halo_a, halo_b, halo_c, halo_d, previous_ref, total_in, proj_ref, _,
    doubled, fields_ref, sums_ref, send_ref,
):
    width = doubled.shape[2] // 2
    lanes = 2 * width
    blocks = pattern_ref.shape[1]
    unpack_halos(where_ref, (halo_a, halo_b, halo_c, halo_d), doubled, blocks, width)
    sums_ref[...] = jnp.zeros_like(sums_ref)
    count = fields_ref.shape[0]
    cells = proj_ref.shape[3]

    def body(q, carry):
        product = applied(pattern_ref, doubled, weights_ref, q, width)
        value = 2.0 * product - previous_ref[q]
        sample = (total_in[q] + COEFFICIENTS[ITERS] * value).astype(BF16)
        fields_ref[:, pl.ds(pl.multiple_of(q * lanes, lanes), lanes)] = sample
        low = lower_half(sample.shape, width)
        zero = jnp.zeros_like(sample)
        left = jnp.concatenate([jnp.where(low, sample, zero), jnp.where(low, zero, sample)], 0)
        right = jnp.concatenate(
            [jnp.concatenate([proj_ref[2 * q + side, o] for side in range(2)], 0) for o in range(proj_ref.shape[1])], 1
        )
        contribution = jnp.dot(left, right, preferred_element_type=F32)
        for side in range(2):
            for o in range(proj_ref.shape[1]):
                slot = slots_ref[o, 2 * q + side]
                sums_ref[slot] += contribution[side * count : (side + 1) * count, o * cells : (o + 1) * cells]
        return carry

    lax.fori_loop(0, blocks // 2, body, 0, unroll=4)
    half = send_ref.shape[0]
    send_ref[...] = sums_ref[half:].astype(BF16)


def halve_kernel(sums_ref, got_ref, out_ref, send_ref):
    half = got_ref.shape[0]
    out_ref[...] = sums_ref[:half] + got_ref[...].astype(F32)
    send_ref[...] = out_ref[half // 2 :].astype(BF16)


def end_kernel(sums_ref, got_ref, out_ref):
    out_ref[...] = sums_ref[: got_ref.shape[0]] + got_ref[...].astype(F32)


def like(*shape, dtype=BF16):
    return jax.ShapeDtypeStruct(shape, dtype)


def swap_edges(block, axis, odd):
    last = lax.axis_size(axis) - 1
    route = [pair for i in range(odd, last, 2) for pair in ((i, i + 1), (i + 1, i))]
    return lax.ppermute(block, axis, route)


def swap_bit(block, axis, bit):
    return lax.ppermute(block, axis, [(i, i ^ bit) for i in range(lax.axis_size(axis))])


def exchange(payloads):
    (a, b, c, d) = payloads
    return (swap_edges(a, "my", 1), swap_edges(b, "mx", 0), swap_edges(c, "mx", 1), swap_edges(d, "my", 0))


def reversed_bits(value, bits):
    out = value * 0
    for b in range(bits):
        out = out + (((value >> b) & 1) << (bits - 1 - b))
    return out


def shards(noise, blocks, pattern, send_lists, proj_weight, tile_of):
    fields, nodes = noise.shape
    count, entries, width, _ = blocks.shape
    nsend = send_lists.shape[1]
    cells = proj_weight.shape[3]
    rows, cols = lax.axis_size("mx"), lax.axis_size("my")
    devices = rows * cols
    i, j = lax.axis_index("mx"), lax.axis_index("my")
    lanes = 2 * width
    pairs = count // 2

    i_odd, j_odd = i % 2, j % 2
    send_row = [3 - j_odd, i_odd, 1 - i_odd, 2 + j_odd]
    take_row = [2 + j_odd, 1 - i_odd, i_odd, 3 - j_odd]
    where = jnp.stack(send_row + take_row).astype(jnp.int32)
    bits = devices.bit_length() - 1
    slots = reversed_bits(tile_of.T, bits) ^ reversed_bits(i * cols + j, bits)
    pattern = pattern.T
    flat = blocks.reshape(count, entries * width, width)

    extended = like(count + 4 * nsend, fields, lanes)
    payload = [like(nsend // 2, fields, lanes)] * 4
    state = like(pairs, fields, lanes, dtype=F32)

    doubled, *sent = pl.pallas_call(
        first_kernel, out_shape=[extended] + payload, in_specs=[SMEM, SMEM, VMEM], out_specs=[VMEM] * 5, compiler_params=PARAMS,
        name="first",
    )(where, send_lists, noise)
    halos = exchange(sent)
    chunk = min(8, count)
    weights = pl.pallas_call(
        weights_kernel, grid=(count // chunk,), out_shape=like(pairs, 2 * entries * width, lanes),
        in_specs=[pl.BlockSpec((chunk, entries * width, width), lambda g: (g, 0, 0))], out_specs=VMEM, compiler_params=PARAMS,
        name="weights",
    )(flat)
    previous, current, total = None, None, None
    for degree in range(1, ITERS):
        inputs = [where, send_lists, pattern, weights, *halos]
        inputs += [noise] if degree == 1 else [noise if degree == 2 else previous, total]
        inputs += [doubled]
        _, following, total, doubled, *sent = pl.pallas_call(
            functools.partial(step_kernel, degree), out_shape=[extended, state, state, extended] + payload,
            in_specs=[SMEM] * 3 + [VMEM] * (len(inputs) - 3), out_specs=[VMEM] * 8,
            input_output_aliases={len(inputs) - 1: 0}, compiler_params=PARAMS, name=f"step{degree}",
        )(*inputs)
        previous, current = current, following
        halos = exchange(sent)
    inputs = [where, pattern, slots, weights, *halos, previous, total, proj_weight, doubled]
    _, sample, sums, send = pl.pallas_call(
        last_kernel,
        out_shape=[extended, like(fields, nodes), like(devices, fields, cells, dtype=F32), like(devices // 2, fields, cells)],
        in_specs=[SMEM] * 3 + [VMEM] * (len(inputs) - 3), out_specs=[VMEM] * 4,
        input_output_aliases={len(inputs) - 1: 0}, compiler_params=PARAMS, name="last",
    )(*inputs)
    stages = [("my", 1 << b) for b in range(cols.bit_length() - 1)] + [("mx", 1 << b) for b in range(rows.bit_length() - 1)]
    for axis, bit in stages[:-1]:
        got = swap_bit(send, axis, bit)
        half = got.shape[0]
        sums, send = pl.pallas_call(
            halve_kernel, out_shape=[like(half, fields, cells, dtype=F32), like(half // 2, fields, cells)],
            in_specs=[VMEM] * 2, out_specs=[VMEM] * 2, compiler_params=PARAMS, name="halve",
        )(sums, got)
    axis, bit = stages[-1]
    got = swap_bit(send, axis, bit)
    tiles = pl.pallas_call(
        end_kernel, out_shape=like(1, fields, cells, dtype=F32), in_specs=[VMEM] * 2, out_specs=VMEM, compiler_params=PARAMS,
        name="end",
    )(sums, got)
    return sample, tiles


def solution(mesh):
    in_specs = (
        P(None, ("mx", "my")),
        P(("mx", "my"), None, None, None),
        P(("mx", "my"), None),
        P(("mx", "my"), None),
        P(("mx", "my"), None, None, None),
        P(("mx", "my"), None),
    )
    out_specs = (P(None, ("mx", "my")), P(("mx", "my"), None, None))
    return jax.shard_map(shards, mesh=mesh, in_specs=in_specs, out_specs=out_specs, check_vma=False)
```

time: 271 us -> 97.9 us (0.36)
  local copies, waits for them, and re-layouts: 74.8 us -> 11.9 us
  waiting for transfers between devices: 68.5 us -> 15.6 us
  matrix products: 37.3 us -> 0 us
  other arithmetic: 26 us -> 0.01 us
  Pallas kernels: 0 us -> 25.7 us
  between operations: 14.5 us -> 0.88 us
  starting transfers between devices: 48.5 us -> 43.2 us
    reduce_scatter x2 -> x0, waiting for transfers between devices: 65.9 us -> none  [the longest x1 34.5 us: shards(): lax.psum_scatter(summed.reshape(count, fields_count, cell_count), 'mx', s...]
    gather x20 -> x0, local copies, waits for them, and re-layouts: 48 us -> none  [the longest x16 25.5 us: extend_blocks(): jnp.take(rounded, send_lists[which], axis=1)]
    dot_general x5 -> x0, matrix products: 37.3 us -> none  [the longest x4 34.6 us: operate(): jnp.einsum('fbkm,bkmn->fbn', columns, blocks, preferred_element_type=jnp....]
    pallas_call x0 -> x11, Pallas kernels: none -> 25.7 us  [the longest x3 14.4 us: shards(): pl.pallas_call(functools.partial(step_kernel, degree), out_shape=[extende...]
    ppermute x16 -> x21, waiting for transfers between devices: 2.6 us -> 15.6 us  [the longest x5 12.4 us: swap_bit(): lax.ppermute(block, axis, [(i, i ^ bit) for i in range(lax.axis_size(axis...]
    select_n x18 -> x0, other arithmetic: 12.1 us -> none  [the longest x16 12.1 us: extend_blocks(): jnp.take(rounded, send_lists[which], axis=1)]
    scatter-add x1 -> x0, other arithmetic: 9.99 us -> none  [shards(): summed = jax.ops.segment_sum(flat, local_ids, count + 1)[:count]]
    reshape x4 -> x0, local copies, waits for them, and re-layouts: 8.74 us -> none  [the longest x2 5.89 us: shards(): noise.astype(jnp.float32).reshape(fields_count, block_count, node_width)]
  transfers between devices with their start and end apart: 18 -> 21, of which waited for: 4 -> 8; matrix products, arithmetic and copies ran while one was open for 10% -> 0% of each run, Pallas kernels for 0% -> 2%
where the time goes in v1:
time: 97.9 us; the launch traced here: 97.4 us
  starting transfers between devices  43.2 us (44%)
  Pallas kernels  25.7 us (26%)
  waiting for transfers between devices  15.6 us (16%)
  local copies, waits for them, and re-layouts  11.9 us (12%)
    ppermute x16, starting transfers between devices, swap_edges(): return lax.ppermute(block, axis, route)  32.7 us
    pallas_call x3, Pallas kernels, shards(): pl.pallas_call(functools.partial(step_kernel, degree), out_shape=[extende...  14.4 us
    ppermute x5, waiting for transfers between devices, swap_bit(): lax.ppermute(block, axis, [(i, i ^ bit) for i in range(lax.axis_size(axis...  12.4 us
    unnamed x28, local copies, waits for them, and re-layouts  11.8 us
    ppermute x5, starting transfers between devices, swap_bit(): lax.ppermute(block, axis, [(i, i ^ bit) for i in range(lax.axis_size(axis...  10.6 us
    pallas_call x1, Pallas kernels, shards(): pl.pallas_call(last_kernel, out_shape=[extended, like(fields, nodes), lik...  8.13 us
    ppermute x16, waiting for transfers between devices, swap_edges(): return lax.ppermute(block, axis, route)  3.27 us
  transfers between devices with their start and end apart: 21, of which 8 were waited for; matrix products, arithmetic and copies ran while one was open for 0% of the time, Pallas kernels for 2%

profile of v1, /device:TPU:0, one launch (start us, length us, event | category | flops | bytes accessed | tf_op | source)
XLA Modules:
  0.0 97.4 jit_solution(15111022580205273771)
XLA Ops:
  0.6 0.1 stack.23.where_ref
  0.7 1.0 %copy-done.3 = bf16[64,4096]{1,0:T(8,128)(2,1)S(1)} copy-done((bf16[64,4096]{1,0:T(8,128)(2,1)S(1)}, bf16[64,4096]{1,0:T(8,128)(2,1)}, u32[]{:S(2)}) %copy-start.3) | copy-done | bytes 524312
  1.8 0.7 copy-done.11
  2.5 0.9 first.1
  3.4 0.7 collective-permute-start
  4.1 3.1 %collective-permute-start.1 = (bf16[8,64,128]{2,1,0:T(8,128)(2,1)S(1)}, bf16[8,64,128]{2,1,0:T(8,128)(2,1)S(1)}, u32[]{:S(2)}, u32[]{:S(2)}) collective-permute-start(bf16[8,64,128]{2,1,0:T(8,128)(2,1)S(1)} %get-tuple-element.39), channel_id=1, source_target_pairs={{0,8},{8,0},{16,24},{24,16},{1,9},{9,1},{17,25},{25,17},{2,10},{10... | collective-permute-start | bytes 393224 | tf_op jit(solution)/shard_map/ppermute | solution.py:157
  7.2 0.7 collective-permute-start.2
  7.9 2.6 %collective-permute-start.3 = (bf16[8,64,128]{2,1,0:T(8,128)(2,1)S(1)}, bf16[8,64,128]{2,1,0:T(8,128)(2,1)S(1)}, u32[]{:S(2)}, u32[]{:S(2)}) collective-permute-start(bf16[8,64,128]{2,1,0:T(8,128)(2,1)S(1)} %get-tuple-element.41), channel_id=1, source_target_pairs={{0,1},{1,0},{2,3},{3,2},{4,5},{5,4},{6,7},{7,6},{8,9},{9,8},{10,11... | collective-permute-start | bytes 393224 | tf_op jit(solution)/shard_map/ppermute | solution.py:157
  10.5 2.8 %copy-done.2 = bf16[64,6,64,64]{3,2,1,0:T(8,128)(2,1)S(1)} copy-done((bf16[64,6,64,64]{3,2,1,0:T(8,128)(2,1)S(1)}, bf16[64,6,64,64]{3,2,1,0:T(8,128)(2,1)}, u32[]{:S(2)}) %copy-start.2) | copy-done | bytes 3145752
  13.3 1.6 %weights.1.weights_ref = bf16[32,768,128]{2,1,0:T(8,128)(2,1)S(1)} custom-call(bf16[64,384,64]{2,1,0:T(8,128)(2,1)S(1)} %bitcast.8), custom_call_target="tpu_custom_call" | custom-call | tf_op jit(solution)/shard_map/weights/pallas_call | solution.py:206
  14.9 0.0 collective-permute-done.1.halo_b
  14.9 0.0 collective-permute-done.2.halo_c
  14.9 4.1 %step1.1 = (bf16[128,64,128]{2,1,0:T(8,128)(2,1)S(1)}, f32[32,64,128]{2,1,0:T(8,128)S(1)}, f32[32,64,128]{2,1,0:T(8,128)S(1)}, bf16[128,64,128]{2,1,0:T(8,128)(2...) custom-call(s32[8]{0:T(128)S(1)} %stack.23.where_ref, ...), custom_call_target="tpu_custom_call", output_to_operand_aliasing={{0}: (9, {})} | custom-call | tf_op jit(solution)/shard_map/step1/pallas_call | solution.py:216
  19.0 1.0 copy-done.6
  20.0 0.7 collective-permute-start.4
  20.6 4.2 %collective-permute-start.5 = (bf16[8,64,128]{2,1,0:T(8,128)(2,1)S(1)}, bf16[8,64,128]{2,1,0:T(8,128)(2,1)S(1)}, u32[]{:S(2)}, u32[]{:S(2)}) collective-permute-start(bf16[8,64,128]{2,1,0:T(8,128)(2,1)S(1)} %get-tuple-element.44), channel_id=1, source_target_pairs={{0,8},{8,0},{16,24},{24,16},{1,9},{9,1},{17,25},{25,17},{2,10},{10... | collective-permute-start | bytes 393224 | tf_op jit(solution)/shard_map/ppermute | solution.py:157
  24.8 0.7 collective-permute-start.6
  25.5 2.6 %collective-permute-start.7 = (bf16[8,64,128]{2,1,0:T(8,128)(2,1)S(1)}, bf16[8,64,128]{2,1,0:T(8,128)(2,1)S(1)}, u32[]{:S(2)}, u32[]{:S(2)}) collective-permute-start(bf16[8,64,128]{2,1,0:T(8,128)(2,1)S(1)} %get-tuple-element.46), channel_id=1, source_target_pairs={{0,1},{1,0},{2,3},{3,2},{4,5},{5,4},{6,7},{7,6},{8,9},{9,8},{10,11... | collective-permute-start | bytes 393224 | tf_op jit(solution)/shard_map/ppermute | solution.py:157
  28.1 1.0 %collective-permute-done.7.halo_d = bf16[8,64,128]{2,1,0:T(8,128)(2,1)S(1)} collective-permute-done((bf16[8,64,128]{2,1,0:T(8,128)(2,1)S(1)}, bf16[8,64,128]{2,1,0:T(8,128)(2,1)S(1)}, u32[]{:S(2)}, u32[]{:S(2)}) %collective-permute-start.7) | collective-permute-done | bytes 131104 | tf_op jit(solution)/shard_map/ppermute | solution.py:157
  29.1 4.9 %step2.1 = (bf16[128,64,128]{2,1,0:T(8,128)(2,1)S(1)}, f32[32,64,128]{2,1,0:T(8,128)S(1)}, f32[32,64,128]{2,1,0:T(8,128)S(1)}, bf16[128,64,128]{2,1,0:T(8,128)(2...) custom-call(s32[8]{0:T(128)S(1)} %stack.23.where_ref, ...), custom_call_target="tpu_custom_call", output_to_operand_aliasing={{0}: (10, {})} | custom-call | tf_op jit(solution)/shard_map/step2/pallas_call | solution.py:216
  34.0 1.1 %copy-done.8 = f32[32,64,128]{2,1,0:T(8,128)} copy-done((f32[32,64,128]{2,1,0:T(8,128)}, f32[32,64,128]{2,1,0:T(8,128)S(1)}, u32[]{:S(2)}) %copy-start.8) | copy-done | bytes 1048600
  35.1 0.7 collective-permute-start.8
  35.8 2.7 %collective-permute-start.9 = (bf16[8,64,128]{2,1,0:T(8,128)(2,1)}, bf16[8,64,128]{2,1,0:T(8,128)(2,1)S(1)}, u32[]{:S(2)}, u32[]{:S(2)}) collective-permute-start(bf16[8,64,128]{2,1,0:T(8,128)(2,1)} %get-tuple-element.50), channel_id=1, source_target_pairs={{0,8},{8,0},{16,24},{24,16},{1,9},{9,1},{17,25},{25,17},{2,10},{10... | collective-permute-start | bytes 393224 | tf_op jit(solution)/shard_map/ppermute | solution.py:157
  38.4 0.7 collective-permute-start.10
  39.1 4.9 %collective-permute-start.11 = (bf16[8,64,128]{2,1,0:T(8,128)(2,1)}, bf16[8,64,128]{2,1,0:T(8,128)(2,1)}, u32[]{:S(2)}, u32[]{:S(2)}) collective-permute-start(bf16[8,64,128]{2,1,0:T(8,128)(2,1)} %get-tuple-element.52), channel_id=1, source_target_pairs={{0,1},{1,0},{2,3},{3,2},{4,5},{5,4},{6,7},{7,6},{8,9},{9,8},{10,11... | collective-permute-start | bytes 393224 | tf_op jit(solution)/shard_map/ppermute | solution.py:157
  44.1 1.3 %collective-permute-done.11.halo_d = bf16[8,64,128]{2,1,0:T(8,128)(2,1)} collective-permute-done((bf16[8,64,128]{2,1,0:T(8,128)(2,1)}, bf16[8,64,128]{2,1,0:T(8,128)(2,1)}, u32[]{:S(2)}, u32[]{:S(2)}) %collective-permute-start.11) | collective-permute-done | bytes 131104 | tf_op jit(solution)/shard_map/ppermute | solution.py:157
  45.4 2.8 %copy-done.1 = bf16[32,768,128]{2,1,0:T(8,128)(2,1)S(1)} copy-done((bf16[32,768,128]{2,1,0:T(8,128)(2,1)S(1)}, bf16[32,768,128]{2,1,0:T(8,128)(2,1)}, u32[]{:S(2)}) %copy-start.1) | copy-done | bytes 6291480
  48.2 1.2 %copy-done.7 = f32[32,64,128]{2,1,0:T(8,128)S(1)} copy-done((f32[32,64,128]{2,1,0:T(8,128)S(1)}, f32[32,64,128]{2,1,0:T(8,128)}, u32[]{:S(2)}) %copy-start.7) | copy-done | bytes 1048600
  49.4 1.2 %copy-done.9 = f32[32,64,128]{2,1,0:T(8,128)S(1)} copy-done((f32[32,64,128]{2,1,0:T(8,128)S(1)}, f32[32,64,128]{2,1,0:T(8,128)}, u32[]{:S(2)}) %copy-start.9) | copy-done | bytes 1048600
  50.6 5.4 %step3.1 = (bf16[128,64,128]{2,1,0:T(8,128)(2,1)S(1)}, f32[32,64,128]{2,1,0:T(8,128)}, f32[32,64,128]{2,1,0:T(8,128)S(1)}, bf16[128,64,128]{2,1,0:T(8,128)(2,1)S...) custom-call(s32[8]{0:T(128)S(1)} %stack.23.where_ref, ...), custom_call_target="tpu_custom_call", output_to_operand_aliasing={{0}: (10, {})} | custom-call | tf_op jit(solution)/shard_map/step3/pallas_call | solution.py:216
  56.0 0.7 collective-permute-start.12
  56.7 1.6 %collective-permute-start.13 = (bf16[8,64,128]{2,1,0:T(8,128)(2,1)S(1)}, bf16[8,64,128]{2,1,0:T(8,128)(2,1)S(1)}, u32[]{:S(2)}, u32[]{:S(2)}) collective-permute-start(bf16[8,64,128]{2,1,0:T(8,128)(2,1)S(1)} %get-tuple-element.57), channel_id=1, source_target_pairs={{0,8},{8,0},{16,24},{24,16},{1,9},{9,1},{17,25},{25,17},{2,10},{10... | collective-permute-start | bytes 393224 | tf_op jit(solution)/shard_map/ppermute | solution.py:157
  58.3 0.7 collective-permute-start.14
  59.0 5.6 %collective-permute-start.15 = (bf16[8,64,128]{2,1,0:T(8,128)(2,1)S(1)}, bf16[8,64,128]{2,1,0:T(8,128)(2,1)S(1)}, u32[]{:S(2)}, u32[]{:S(2)}) collective-permute-start(bf16[8,64,128]{2,1,0:T(8,128)(2,1)S(1)} %get-tuple-element.59), channel_id=1, source_target_pairs={{0,1},{1,0},{2,3},{3,2},{4,5},{5,4},{6,7},{7,6},{8,9},{9,8},{10,11... | collective-permute-start | bytes 393224 | tf_op jit(solution)/shard_map/ppermute | solution.py:157
  64.6 0.9 collective-permute-done.15.halo_d
  65.5 8.1 %last.1 = (bf16[128,64,128]{2,1,0:T(8,128)(2,1)S(1)}, bf16[64,4096]{1,0:T(8,128)(2,1)}, f32[32,64,128]{2,1,0:T(8,128)S(1)}, bf16[16,64,128]{2,1,0:T(8,128)(2,1)S(1)}) custom-call(s32[8]{0:T(128)S(1)} %stack.23.where_ref, s32[6,64]{1,0:T(8,128)S(1)} %bitcast.12, s32[2,64]{1,0:T(2,128)S(1)} %xor_bitcast_fusion.slots_ref, ...), custom_call_target="tpu_custom_call", output_to_operand_aliasing={{0}: (11, {})} | custom-call | tf_op jit(solution)/shard_map/last/pallas_call | solution.py:224
  73.7 0.7 collective-permute-start.16
  74.3 1.2 %collective-permute-done.16.got_ref = bf16[16,64,128]{2,1,0:T(8,128)(2,1)S(1)} collective-permute-done((bf16[16,64,128]{2,1,0:T(8,128)(2,1)S(1)}, bf16[16,64,128]{2,1,0:T(8,128)(2,1)S(1)}, u32[]{:S(2)}, u32[]{:S(2)}) %collective-permute-start.16) | collective-permute-done | bytes 262176 | tf_op jit(solution)/shard_map/ppermute | solution.py:161
  75.5 0.1 halve.4
  75.6 2.2 %collective-permute-start.17 = (bf16[8,64,128]{2,1,0:T(8,128)(2,1)S(1)}, bf16[8,64,128]{2,1,0:T(8,128)(2,1)S(1)}, u32[]{:S(2)}, u32[]{:S(2)}) collective-permute-start(bf16[8,64,128]{2,1,0:T(8,128)(2,1)S(1)} %get-tuple-element.67), channel_id=1, source_target_pairs={{0,2},{1,3},{2,0},{3,1},{4,6},{5,7},{6,4},{7,5},{8,10},{9,11},{10,... | collective-permute-start | bytes 393224 | tf_op jit(solution)/shard_map/ppermute | solution.py:161
  77.8 4.0 %collective-permute-done.17.got_ref = bf16[8,64,128]{2,1,0:T(8,128)(2,1)S(1)} collective-permute-done((bf16[8,64,128]{2,1,0:T(8,128)(2,1)S(1)}, bf16[8,64,128]{2,1,0:T(8,128)(2,1)S(1)}, u32[]{:S(2)}, u32[]{:S(2)}) %collective-permute-start.17) | collective-permute-done | bytes 131104 | tf_op jit(solution)/shard_map/ppermute | solution.py:161
  81.8 2.1 %collective-permute-start.18 = (bf16[4,64,128]{2,1,0:T(8,128)(2,1)S(1)}, bf16[4,64,128]{2,1,0:T(8,128)(2,1)S(1)}, u32[]{:S(2)}, u32[]{:S(2)}) collective-permute-start(bf16[4,64,128]{2,1,0:T(8,128)(2,1)S(1)} %get-tuple-element.69), channel_id=1, source_target_pairs={{0,4},{1,5},{2,6},{3,7},{4,0},{5,1},{6,2},{7,3},{8,12},{9,13},{10,... | collective-permute-start | bytes 196616 | tf_op jit(solution)/shard_map/ppermute | solution.py:161
  83.9 2.3 %collective-permute-done.18.got_ref = bf16[4,64,128]{2,1,0:T(8,128)(2,1)S(1)} collective-permute-done((bf16[4,64,128]{2,1,0:T(8,128)(2,1)S(1)}, bf16[4,64,128]{2,1,0:T(8,128)(2,1)S(1)}, u32[]{:S(2)}, u32[]{:S(2)}) %collective-permute-start.18) | collective-permute-done | bytes 65568 | tf_op jit(solution)/shard_map/ppermute | solution.py:161
  86.2 4.0 %collective-permute-start.19 = (bf16[2,64,128]{2,1,0:T(8,128)(2,1)S(1)}, bf16[2,64,128]{2,1,0:T(8,128)(2,1)S(1)}, u32[]{:S(2)}, u32[]{:S(2)}) collective-permute-start(bf16[2,64,128]{2,1,0:T(8,128)(2,1)S(1)} %get-tuple-element.71), channel_id=1, source_target_pairs={{0,8},{8,0},{16,24},{24,16},{1,9},{9,1},{17,25},{25,17},{2,10},{10... | collective-permute-start | bytes 98312 | tf_op jit(solution)/shard_map/ppermute | solution.py:161
  90.1 1.9 %collective-permute-done.19.got_ref = bf16[2,64,128]{2,1,0:T(8,128)(2,1)S(1)} collective-permute-done((bf16[2,64,128]{2,1,0:T(8,128)(2,1)S(1)}, bf16[2,64,128]{2,1,0:T(8,128)(2,1)S(1)}, u32[]{:S(2)}, u32[]{:S(2)}) %collective-permute-start.19) | collective-permute-done | bytes 32800 | tf_op jit(solution)/shard_map/ppermute | solution.py:161
  92.1 1.7 %collective-permute-start.20 = (bf16[1,64,128]{2,1,0:T(8,128)(2,1)S(1)}, bf16[1,64,128]{2,1,0:T(8,128)(2,1)S(1)}, u32[]{:S(2)}, u32[]{:S(2)}) collective-permute-start(bf16[1,64,128]{2,1,0:T(8,128)(2,1)S(1)} %get-tuple-element.73), channel_id=1, source_target_pairs={{0,16},{8,24},{16,0},{24,8},{1,17},{9,25},{17,1},{25,9},{2,18},{10... | collective-permute-start | bytes 49160 | tf_op jit(solution)/shard_map/ppermute | solution.py:161
  93.7 3.0 %collective-permute-done.20.got_ref = bf16[1,64,128]{2,1,0:T(8,128)(2,1)S(1)} collective-permute-done((bf16[1,64,128]{2,1,0:T(8,128)(2,1)S(1)}, bf16[1,64,128]{2,1,0:T(8,128)(2,1)S(1)}, u32[]{:S(2)}, u32[]{:S(2)}) %collective-permute-start.20) | collective-permute-done | bytes 16416 | tf_op jit(solution)/shard_map/ppermute | solution.py:161
  96.8 0.6 end.1
  (35 shorter events, 0.1 us)
Async XLA Ops:
  0.7 1.0 %copy-start.3 = (bf16[64,4096]{1,0:T(8,128)(2,1)S(1)}, bf16[64,4096]{1,0:T(8,128)(2,1)}, u32[]{:S(2)}) copy-start(bf16[64,4096]{1,0:T(8,128)(2,1)} %rest_0_.3) | copy-start | bytes 1572868
  1.8 0.7 copy-start.11
  3.4 11.5 %collective-permute-start = (bf16[8,64,128]{2,1,0:T(8,128)(2,1)S(1)}, bf16[8,64,128]{2,1,0:T(8,128)(2,1)S(1)}, u32[]{:S(2)}, u32[]{:S(2)}) collective-permute-start(bf16[8,64,128]{2,1,0:T(8,128)(2,1)S(1)} %get-tuple-element.38), channel_id=1, source_target_pairs={{1,2},{2,1},{3,4},{4,3},{5,6},{6,5},{9,10},{10,9},{11,12},{12,11},... | collective-permute-start | bytes 393224 | tf_op jit(solution)/shard_map/ppermute | solution.py:157
  4.1 10.8 %collective-permute-start.1 = (bf16[8,64,128]{2,1,0:T(8,128)(2,1)S(1)}, bf16[8,64,128]{2,1,0:T(8,128)(2,1)S(1)}, u32[]{:S(2)}, u32[]{:S(2)}) collective-permute-start(bf16[8,64,128]{2,1,0:T(8,128)(2,1)S(1)} %get-tuple-element.39), channel_id=1, source_target_pairs={{0,8},{8,0},{16,24},{24,16},{1,9},{9,1},{17,25},{25,17},{2,10},{10... | collective-permute-start | bytes 393224 | tf_op jit(solution)/shard_map/ppermute | solution.py:157
  7.2 7.7 %collective-permute-start.2 = (bf16[8,64,128]{2,1,0:T(8,128)(2,1)S(1)}, bf16[8,64,128]{2,1,0:T(8,128)(2,1)S(1)}, u32[]{:S(2)}, u32[]{:S(2)}) collective-permute-start(bf16[8,64,128]{2,1,0:T(8,128)(2,1)S(1)} %get-tuple-element.40), channel_id=1, source_target_pairs={{8,16},{16,8},{9,17},{17,9},{10,18},{18,10},{11,19},{19,11},{12,20... | collective-permute-start | bytes 393224 | tf_op jit(solution)/shard_map/ppermute | solution.py:157
  7.9 7.0 %collective-permute-start.3 = (bf16[8,64,128]{2,1,0:T(8,128)(2,1)S(1)}, bf16[8,64,128]{2,1,0:T(8,128)(2,1)S(1)}, u32[]{:S(2)}, u32[]{:S(2)}) collective-permute-start(bf16[8,64,128]{2,1,0:T(8,128)(2,1)S(1)} %get-tuple-element.41), channel_id=1, source_target_pairs={{0,1},{1,0},{2,3},{3,2},{4,5},{5,4},{6,7},{7,6},{8,9},{9,8},{10,11... | collective-permute-start | bytes 393224 | tf_op jit(solution)/shard_map/ppermute | solution.py:157
  10.5 2.8 %copy-start.2 = (bf16[64,6,64,64]{3,2,1,0:T(8,128)(2,1)S(1)}, bf16[64,6,64,64]{3,2,1,0:T(8,128)(2,1)}, u32[]{:S(2)}) copy-start(bf16[64,6,64,64]{3,2,1,0:T(8,128)(2,1)} %param.7) | copy-start | bytes 9437188
  13.3 1.6 %copy-start.4 = (bf16[64,4096]{1,0:T(8,128)(2,1)S(1)}, bf16[64,4096]{1,0:T(8,128)(2,1)}, u32[]{:S(2)}) copy-start(bf16[64,4096]{1,0:T(8,128)(2,1)} %rest_0_.3) | copy-start | bytes 1572868
  13.3 1.6 %copy-start.10 = (s32[64,6]{0,1:T(8,128)S(1)}, s32[64,6]{0,1:T(8,128)}, u32[]{:S(2)}) copy-start(s32[64,6]{0,1:T(8,128)} %param.8) | copy-start | bytes 4612
  13.3 1.6 %copy-start.12 = (s32[4,16]{1,0:T(4,128)S(1)}, s32[4,16]{1,0:T(4,128)}, u32[]{:S(2)}) copy-start(s32[4,16]{1,0:T(4,128)} %sends_ref.7) | copy-start | bytes 772
  14.8 14.3 %copy-start = (bf16[32,768,128]{2,1,0:T(8,128)(2,1)}, bf16[32,768,128]{2,1,0:T(8,128)(2,1)S(1)}, u32[]{:S(2)}) copy-start(bf16[32,768,128]{2,1,0:T(8,128)(2,1)S(1)} %weights.1.weights_ref) | copy-start | bytes 18874372
  19.0 1.0 %copy-start.6 = (f32[32,64,128]{2,1,0:T(8,128)}, f32[32,64,128]{2,1,0:T(8,128)S(1)}, u32[]{:S(2)}) copy-start(f32[32,64,128]{2,1,0:T(8,128)S(1)} %get-tuple-element.53.rest_0_) | copy-start | bytes 3145732
  20.0 8.1 %collective-permute-start.4 = (bf16[8,64,128]{2,1,0:T(8,128)(2,1)S(1)}, bf16[8,64,128]{2,1,0:T(8,128)(2,1)S(1)}, u32[]{:S(2)}, u32[]{:S(2)}) collective-permute-start(bf16[8,64,128]{2,1,0:T(8,128)(2,1)S(1)} %get-tuple-element.43), channel_id=1, source_target_pairs={{1,2},{2,1},{3,4},{4,3},{5,6},{6,5},{9,10},{10,9},{11,12},{12,11},... | collective-permute-start | bytes 393224 | tf_op jit(solution)/shard_map/ppermute | solution.py:157
  20.6 7.5 %collective-permute-start.5 = (bf16[8,64,128]{2,1,0:T(8,128)(2,1)S(1)}, bf16[8,64,128]{2,1,0:T(8,128)(2,1)S(1)}, u32[]{:S(2)}, u32[]{:S(2)}) collective-permute-start(bf16[8,64,128]{2,1,0:T(8,128)(2,1)S(1)} %get-tuple-element.44), channel_id=1, source_target_pairs={{0,8},{8,0},{16,24},{24,16},{1,9},{9,1},{17,25},{25,17},{2,10},{10... | collective-permute-start | bytes 393224 | tf_op jit(solution)/shard_map/ppermute | solution.py:157
  24.8 3.3 %collective-permute-start.6 = (bf16[8,64,128]{2,1,0:T(8,128)(2,1)S(1)}, bf16[8,64,128]{2,1,0:T(8,128)(2,1)S(1)}, u32[]{:S(2)}, u32[]{:S(2)}) collective-permute-start(bf16[8,64,128]{2,1,0:T(8,128)(2,1)S(1)} %get-tuple-element.45), channel_id=1, source_target_pairs={{8,16},{16,8},{9,17},{17,9},{10,18},{18,10},{11,19},{19,11},{12,20... | collective-permute-start | bytes 393224 | tf_op jit(solution)/shard_map/ppermute | solution.py:157
  25.5 3.6 %collective-permute-start.7 = (bf16[8,64,128]{2,1,0:T(8,128)(2,1)S(1)}, bf16[8,64,128]{2,1,0:T(8,128)(2,1)S(1)}, u32[]{:S(2)}, u32[]{:S(2)}) collective-permute-start(bf16[8,64,128]{2,1,0:T(8,128)(2,1)S(1)} %get-tuple-element.46), channel_id=1, source_target_pairs={{0,1},{1,0},{2,3},{3,2},{4,5},{5,4},{6,7},{7,6},{8,9},{9,8},{10,11... | collective-permute-start | bytes 393224 | tf_op jit(solution)/shard_map/ppermute | solution.py:157
  34.0 1.1 %copy-start.8 = (f32[32,64,128]{2,1,0:T(8,128)}, f32[32,64,128]{2,1,0:T(8,128)S(1)}, u32[]{:S(2)}) copy-start(f32[32,64,128]{2,1,0:T(8,128)S(1)} %get-tuple-element.54.rest_1_) | copy-start | bytes 3145732
  35.1 9.0 %collective-permute-start.8 = (bf16[8,64,128]{2,1,0:T(8,128)(2,1)}, bf16[8,64,128]{2,1,0:T(8,128)(2,1)S(1)}, u32[]{:S(2)}, u32[]{:S(2)}) collective-permute-start(bf16[8,64,128]{2,1,0:T(8,128)(2,1)} %get-tuple-element.49), channel_id=1, source_target_pairs={{1,2},{2,1},{3,4},{4,3},{5,6},{6,5},{9,10},{10,9},{11,12},{12,11},... | collective-permute-start | bytes 393224 | tf_op jit(solution)/shard_map/ppermute | solution.py:157
  35.8 8.3 %collective-permute-start.9 = (bf16[8,64,128]{2,1,0:T(8,128)(2,1)}, bf16[8,64,128]{2,1,0:T(8,128)(2,1)S(1)}, u32[]{:S(2)}, u32[]{:S(2)}) collective-permute-start(bf16[8,64,128]{2,1,0:T(8,128)(2,1)} %get-tuple-element.50), channel_id=1, source_target_pairs={{0,8},{8,0},{16,24},{24,16},{1,9},{9,1},{17,25},{25,17},{2,10},{10... | collective-permute-start | bytes 393224 | tf_op jit(solution)/shard_map/ppermute | solution.py:157
  38.4 5.6 %collective-permute-start.10 = (bf16[8,64,128]{2,1,0:T(8,128)(2,1)}, bf16[8,64,128]{2,1,0:T(8,128)(2,1)S(1)}, u32[]{:S(2)}, u32[]{:S(2)}) collective-permute-start(bf16[8,64,128]{2,1,0:T(8,128)(2,1)} %get-tuple-element.51), channel_id=1, source_target_pairs={{8,16},{16,8},{9,17},{17,9},{10,18},{18,10},{11,19},{19,11},{12,20... | collective-permute-start | bytes 393224 | tf_op jit(solution)/shard_map/ppermute | solution.py:157
  39.1 6.3 %collective-permute-start.11 = (bf16[8,64,128]{2,1,0:T(8,128)(2,1)}, bf16[8,64,128]{2,1,0:T(8,128)(2,1)}, u32[]{:S(2)}, u32[]{:S(2)}) collective-permute-start(bf16[8,64,128]{2,1,0:T(8,128)(2,1)} %get-tuple-element.52), channel_id=1, source_target_pairs={{0,1},{1,0},{2,3},{3,2},{4,5},{5,4},{6,7},{7,6},{8,9},{9,8},{10,11... | collective-permute-start | bytes 393224 | tf_op jit(solution)/shard_map/ppermute | solution.py:157
  45.4 2.8 %copy-start.1 = (bf16[32,768,128]{2,1,0:T(8,128)(2,1)S(1)}, bf16[32,768,128]{2,1,0:T(8,128)(2,1)}, u32[]{:S(2)}) copy-start(bf16[32,768,128]{2,1,0:T(8,128)(2,1)} %copy-done) | copy-start | bytes 18874372
  48.2 1.2 %copy-start.7 = (f32[32,64,128]{2,1,0:T(8,128)S(1)}, f32[32,64,128]{2,1,0:T(8,128)}, u32[]{:S(2)}) copy-start(f32[32,64,128]{2,1,0:T(8,128)} %copy-done.6) | copy-start | bytes 3145732
  49.4 1.2 %copy-start.9 = (f32[32,64,128]{2,1,0:T(8,128)S(1)}, f32[32,64,128]{2,1,0:T(8,128)}, u32[]{:S(2)}) copy-start(f32[32,64,128]{2,1,0:T(8,128)} %copy-done.8) | copy-start | bytes 3145732
  50.6 14.0 %copy-start.13 = (s32[64,2]{0,1:T(2,128)S(1)}, s32[64,2]{0,1:T(2,128)}, u32[]{:S(2)}) copy-start(s32[64,2]{0,1:T(2,128)} %param.11) | copy-start | bytes 1540
  50.6 14.9 %copy-start.5 = (bf16[64,2,64,128]{3,2,1,0:T(8,128)(2,1)S(1)}, bf16[64,2,64,128]{3,2,1,0:T(8,128)(2,1)}, u32[]{:S(2)}) copy-start(bf16[64,2,64,128]{3,2,1,0:T(8,128)(2,1)} %proj_ref.1) | copy-start | bytes 6291460
  56.0 8.6 %collective-permute-start.12 = (bf16[8,64,128]{2,1,0:T(8,128)(2,1)S(1)}, bf16[8,64,128]{2,1,0:T(8,128)(2,1)S(1)}, u32[]{:S(2)}, u32[]{:S(2)}) collective-permute-start(bf16[8,64,128]{2,1,0:T(8,128)(2,1)S(1)} %get-tuple-element.56), channel_id=1, source_target_pairs={{1,2},{2,1},{3,4},{4,3},{5,6},{6,5},{9,10},{10,9},{11,12},{12,11},... | collective-permute-start | bytes 393224 | tf_op jit(solution)/shard_map/ppermute | solution.py:157
  56.7 7.9 %collective-permute-start.13 = (bf16[8,64,128]{2,1,0:T(8,128)(2,1)S(1)}, bf16[8,64,128]{2,1,0:T(8,128)(2,1)S(1)}, u32[]{:S(2)}, u32[]{:S(2)}) collective-permute-start(bf16[8,64,128]{2,1,0:T(8,128)(2,1)S(1)} %get-tuple-element.57), channel_id=1, source_target_pairs={{0,8},{8,0},{16,24},{24,16},{1,9},{9,1},{17,25},{25,17},{2,10},{10... | collective-permute-start | bytes 393224 | tf_op jit(solution)/shard_map/ppermute | solution.py:157
  58.3 6.3 %collective-permute-start.14 = (bf16[8,64,128]{2,1,0:T(8,128)(2,1)S(1)}, bf16[8,64,128]{2,1,0:T(8,128)(2,1)S(1)}, u32[]{:S(2)}, u32[]{:S(2)}) collective-permute-start(bf16[8,64,128]{2,1,0:T(8,128)(2,1)S(1)} %get-tuple-element.58), channel_id=1, source_target_pairs={{8,16},{16,8},{9,17},{17,9},{10,18},{18,10},{11,19},{19,11},{12,20... | collective-permute-start | bytes 393224 | tf_op jit(solution)/shard_map/ppermute | solution.py:157
  59.0 6.6 %collective-permute-start.15 = (bf16[8,64,128]{2,1,0:T(8,128)(2,1)S(1)}, bf16[8,64,128]{2,1,0:T(8,128)(2,1)S(1)}, u32[]{:S(2)}, u32[]{:S(2)}) collective-permute-start(bf16[8,64,128]{2,1,0:T(8,128)(2,1)S(1)} %get-tuple-element.59), channel_id=1, source_target_pairs={{0,1},{1,0},{2,3},{3,2},{4,5},{5,4},{6,7},{7,6},{8,9},{9,8},{10,11... | collective-permute-start | bytes 393224 | tf_op jit(solution)/shard_map/ppermute | solution.py:157
  73.7 1.8 %collective-permute-start.16 = (bf16[16,64,128]{2,1,0:T(8,128)(2,1)S(1)}, bf16[16,64,128]{2,1,0:T(8,128)(2,1)S(1)}, u32[]{:S(2)}, u32[]{:S(2)}) collective-permute-start(bf16[16,64,128]{2,1,0:T(8,128)(2,1)S(1)} %get-tuple-element.65), channel_id=1, source_target_pairs={{0,1},{1,0},{2,3},{3,2},{4,5},{5,4},{6,7},{7,6},{8,9},{9,8},{10,11... | collective-permute-start | bytes 786440 | tf_op jit(solution)/shard_map/ppermute | solution.py:161
  75.6 6.2 %collective-permute-start.17 = (bf16[8,64,128]{2,1,0:T(8,128)(2,1)S(1)}, bf16[8,64,128]{2,1,0:T(8,128)(2,1)S(1)}, u32[]{:S(2)}, u32[]{:S(2)}) collective-permute-start(bf16[8,64,128]{2,1,0:T(8,128)(2,1)S(1)} %get-tuple-element.67), channel_id=1, source_target_pairs={{0,2},{1,3},{2,0},{3,1},{4,6},{5,7},{6,4},{7,5},{8,10},{9,11},{10,... | collective-permute-start | bytes 393224 | tf_op jit(solution)/shard_map/ppermute | solution.py:161
  81.8 4.3 %collective-permute-start.18 = (bf16[4,64,128]{2,1,0:T(8,128)(2,1)S(1)}, bf16[4,64,128]{2,1,0:T(8,128)(2,1)S(1)}, u32[]{:S(2)}, u32[]{:S(2)}) collective-permute-start(bf16[4,64,128]{2,1,0:T(8,128)(2,1)S(1)} %get-tuple-element.69), channel_id=1, source_target_pairs={{0,4},{1,5},{2,6},{3,7},{4,0},{5,1},{6,2},{7,3},{8,12},{9,13},{10,... | collective-permute-start | bytes 196616 | tf_op jit(solution)/shard_map/ppermute | solution.py:161
  86.2 5.9 %collective-permute-start.19 = (bf16[2,64,128]{2,1,0:T(8,128)(2,1)S(1)}, bf16[2,64,128]{2,1,0:T(8,128)(2,1)S(1)}, u32[]{:S(2)}, u32[]{:S(2)}) collective-permute-start(bf16[2,64,128]{2,1,0:T(8,128)(2,1)S(1)} %get-tuple-element.71), channel_id=1, source_target_pairs={{0,8},{8,0},{16,24},{24,16},{1,9},{9,1},{17,25},{25,17},{2,10},{10... | collective-permute-start | bytes 98312 | tf_op jit(solution)/shard_map/ppermute | solution.py:161
  92.1 4.7 %collective-permute-start.20 = (bf16[1,64,128]{2,1,0:T(8,128)(2,1)S(1)}, bf16[1,64,128]{2,1,0:T(8,128)(2,1)S(1)}, u32[]{:S(2)}, u32[]{:S(2)}) collective-permute-start(bf16[1,64,128]{2,1,0:T(8,128)(2,1)S(1)} %get-tuple-element.73), channel_id=1, source_target_pairs={{0,16},{8,24},{16,0},{24,8},{1,17},{9,25},{17,1},{25,9},{2,18},{10... | collective-permute-start | bytes 49160 | tf_op jit(solution)/shard_map/ppermute | solution.py:161

commit v2 on v1

v2 whole, which is shorter than its diff:
```python
import functools

import jax
import jax.numpy as jnp
from jax import lax
from jax.experimental import pallas as pl
from jax.experimental.pallas import tpu as pltpu
from jax.sharding import PartitionSpec as P

ITERS = 4
COEFFICIENTS = (0.8, 0.6, -0.45, 0.35, -0.3)
VMEM = pl.BlockSpec(memory_space=pltpu.VMEM)
SMEM = pl.BlockSpec(memory_space=pltpu.SMEM)
PARAMS = pltpu.CompilerParams(vmem_limit_bytes=8 << 20)
BF16 = jnp.bfloat16
F32 = jnp.float32


def lower_half(shape, width):
    return lax.broadcasted_iota(jnp.int32, shape, len(shape) - 1) < width


def both_halves(pair, width):
    first, second = pair[:, :width], pair[:, width:]
    return jnp.concatenate([first, first], 1), jnp.concatenate([second, second], 1)


def side_by_side(doubled, one, two, width):
    a, b = doubled[one], doubled[two]
    return jnp.where(lower_half(a.shape, width), a, b)


def plan():
    i, j = lax.axis_index("mx"), lax.axis_index("my")
    rows, cols = lax.axis_size("mx"), lax.axis_size("my")
    i_odd, j_odd = i & 1, j & 1
    sent = (3 - j_odd, i_odd, 1 - i_odd, 2 + j_odd)
    place = (2 + j_odd, 1 - i_odd, i_odd, 3 - j_odd)
    real = ((j > 0) & (j < cols - 1), None, (i > 0) & (i < rows - 1), None)
    return sent, place, real


def fill_payloads(sends_ref, doubled, payloads, width):
    for row, payload in zip(plan()[0], payloads):
        for q in range(payload.shape[0]):
            payload[q] = side_by_side(doubled, sends_ref[row, 2 * q], sends_ref[row, 2 * q + 1], width)


def first_kernel(sends_ref, noise_ref, doubled, *payloads):
    fields, nodes = noise_ref.shape
    lanes = doubled.shape[2]
    width = lanes // 2
    for q in range(nodes // lanes):
        doubled[2 * q], doubled[2 * q + 1] = both_halves(noise_ref[:, q * lanes : (q + 1) * lanes], width)
    fill_payloads(sends_ref, doubled, payloads, width)


def weights_kernel(blocks_ref, out_ref):
    step = pl.program_id(0)
    pairs = blocks_ref.shape[0] // 2
    depth, width = blocks_ref.shape[1:]
    zero = jnp.zeros((depth, width), BF16)
    for r in range(pairs):
        out_ref[step * pairs + r, :depth] = jnp.concatenate([blocks_ref[2 * r], zero], 1)
        out_ref[step * pairs + r, depth:] = jnp.concatenate([zero, blocks_ref[2 * r + 1]], 1)


def unpack_halos(halos, doubled, base, width):
    _, places, reals = plan()
    for halo, place, real in zip(halos, places, reals):
        count = 2 * halo.shape[0]
        start = base + place * count
        for q in range(halo.shape[0]):
            pair = halo[q]
            if real is not None:
                pair = jnp.where(real, pair, jnp.zeros_like(pair))
            doubled[start + 2 * q], doubled[start + 2 * q + 1] = both_halves(pair, width)


def applied(pattern_ref, doubled, weights_ref, q, width):
    entries = pattern_ref.shape[0]
    wanted = [pattern_ref[k, 2 * q + side] for side in range(2) for k in range(entries)]
    columns = [side_by_side(doubled, wanted[k], wanted[k + 1], width) for k in range(0, 2 * entries, 2)]
    return jnp.dot(jnp.concatenate(columns, 1), weights_ref[q], preferred_element_type=F32)


def step_kernel(degree, sends_ref, pattern_ref, weights_ref, halo_a, halo_b, halo_c, halo_d, *rest):
    if degree == 1:
        noise_ref, _, doubled, current_ref, total_ref, following, *payloads = rest
    else:
        previous_ref, total_in, _, doubled, current_ref, total_ref, following, *payloads = rest
    width = doubled.shape[2] // 2
    lanes = 2 * width
    blocks = pattern_ref.shape[1]
    unpack_halos((halo_a, halo_b, halo_c, halo_d), doubled, blocks, width)

    def body(q, carry):
        product = applied(pattern_ref, doubled, weights_ref, q, width)
        if degree == 1:
            start = noise_ref[:, pl.ds(pl.multiple_of(q * lanes, lanes), lanes)].astype(F32)
            value = product
            total_ref[q] = COEFFICIENTS[0] * start + COEFFICIENTS[1] * value
        else:
            if degree == 2:
                start = previous_ref[:, pl.ds(pl.multiple_of(q * lanes, lanes), lanes)].astype(F32)
            else:
                start = previous_ref[q]
            value = 2.0 * product - start
            total_ref[q] = total_in[q] + COEFFICIENTS[degree] * value
        current_ref[q] = value
        following[2 * q], following[2 * q + 1] = both_halves(value.astype(BF16), width)
        return carry

    lax.fori_loop(0, blocks // 2, body, 0, unroll=16)
    fill_payloads(sends_ref, following, payloads, width)


def last_kernel(
    pattern_ref, tiles_ref, weights_ref, halo_a, halo_b, halo_c, halo_d, previous_ref, total_in, proj_ref, _,
    doubled, fields_ref, sums_ref, send_ref,
):
    width = doubled.shape[2] // 2
    lanes = 2 * width
    blocks = pattern_ref.shape[1]
    unpack_halos((halo_a, halo_b, halo_c, halo_d), doubled, blocks, width)
    sums_ref[...] = jnp.zeros_like(sums_ref)
    count = fields_ref.shape[0]
    cells = proj_ref.shape[3]
    core = lax.axis_index("my") & 1
    half = send_ref.shape[0]

    def body(q, carry):
        product = applied(pattern_ref, doubled, weights_ref, q, width)
        value = 2.0 * product - previous_ref[q]
        sample = (total_in[q] + COEFFICIENTS[ITERS] * value).astype(BF16)
        fields_ref[:, pl.ds(pl.multiple_of(q * lanes, lanes), lanes)] = sample
        low = lower_half(sample.shape, width)
        zero = jnp.zeros_like(sample)
        left = jnp.concatenate([jnp.where(low, sample, zero), jnp.where(low, zero, sample)], 0)
        right = jnp.concatenate(
            [jnp.concatenate([proj_ref[2 * q + side, o] for side in range(2)], 0) for o in range(proj_ref.shape[1])], 1
        )
        contribution = jnp.dot(left, right, preferred_element_type=F32)
        for side in range(2):
            for o in range(proj_ref.shape[1]):
                tile = tiles_ref[o, 2 * q + side]
                slot = ((tile ^ core) & 1) * half + (tile >> 1)
                sums_ref[slot] += contribution[side * count : (side + 1) * count, o * cells : (o + 1) * cells]
        return carry

    lax.fori_loop(0, blocks // 2, body, 0, unroll=16)
    send_ref[...] = sums_ref[half:].astype(BF16)


def join_kernel(sums_ref, got_ref, out_ref):
    out_ref[...] = (sums_ref[: got_ref.shape[0]] + got_ref[...].astype(F32)).astype(BF16)


def end_kernel(parts_ref, out_ref):
    out_ref[0] = jnp.sum(parts_ref[...].astype(F32), axis=0)


def like(*shape, dtype=BF16):
    return jax.ShapeDtypeStruct(shape, dtype)


def swap(block, partner):
    rows, cols = lax.axis_size("mx"), lax.axis_size("my")
    route = []
    for i in range(rows):
        for j in range(cols):
            a, b = partner(i, j)
            route.append((i * cols + j, a * cols + b))
    return lax.ppermute(block, ("mx", "my"), route)


def exchange(payloads):
    rows, cols = lax.axis_size("mx"), lax.axis_size("my")

    def odd_cols(i, j):
        return i, ((j + 1) if j % 2 else (j - 1)) % cols

    def even_rows(i, j):
        return i ^ 1, j

    def odd_rows(i, j):
        if i in (0, rows - 1):
            return i, j ^ 1
        return (i + 1 if i % 2 else i - 1), j

    def even_cols(i, j):
        return i, j ^ 1

    return [swap(block, partner) for block, partner in zip(payloads, (odd_cols, even_rows, odd_rows, even_cols))]


def shards(noise, blocks, pattern, send_lists, proj_weight, tile_of):
    fields, nodes = noise.shape
    count, entries, width, _ = blocks.shape
    nsend = send_lists.shape[1]
    cells = proj_weight.shape[3]
    rows, cols = lax.axis_size("mx"), lax.axis_size("my")
    devices = rows * cols
    lanes = 2 * width
    pairs = count // 2
    pattern = pattern.T
    flat = blocks.reshape(count, entries * width, width)

    extended = like(count + 4 * nsend, fields, lanes)
    payload = [like(nsend // 2, fields, lanes)] * 4
    state = like(pairs, fields, lanes, dtype=F32)

    doubled, *sent = pl.pallas_call(
        first_kernel, out_shape=[extended] + payload, in_specs=[SMEM, VMEM], out_specs=[VMEM] * 5, compiler_params=PARAMS,
        name="first",
    )(send_lists, noise)
    halos = exchange(sent)
    chunk = min(8, count)
    weights = pl.pallas_call(
        weights_kernel, grid=(count // chunk,), out_shape=like(pairs, 2 * entries * width, lanes),
        in_specs=[pl.BlockSpec((chunk, entries * width, width), lambda g: (g, 0, 0))], out_specs=VMEM, compiler_params=PARAMS,
        name="weights",
    )(flat)
    previous, current, total = None, None, None
    for degree in range(1, ITERS):
        inputs = [send_lists, pattern, weights, *halos]
        inputs += [noise] if degree == 1 else [noise if degree == 2 else previous, total]
        inputs += [doubled]
        _, following, total, doubled, *sent = pl.pallas_call(
            functools.partial(step_kernel, degree), out_shape=[extended, state, state, extended] + payload,
            in_specs=[SMEM] * 2 + [VMEM] * (len(inputs) - 2), out_specs=[VMEM] * 8,
            input_output_aliases={len(inputs) - 1: 0}, compiler_params=PARAMS, name=f"step{degree}",
        )(*inputs)
        previous, current = current, following
        halos = exchange(sent)
    inputs = [pattern, tile_of.T, weights, *halos, previous, total, proj_weight, doubled]
    _, sample, sums, send = pl.pallas_call(
        last_kernel,
        out_shape=[extended, like(fields, nodes), like(devices, fields, cells, dtype=F32), like(devices // 2, fields, cells)],
        in_specs=[SMEM] * 2 + [VMEM] * (len(inputs) - 2), out_specs=[VMEM] * 4,
        input_output_aliases={len(inputs) - 1: 0}, compiler_params=PARAMS, name="last",
    )(*inputs)
    got = swap(send, lambda i, j: (i, j ^ 1))
    joined = pl.pallas_call(
        join_kernel, out_shape=like(devices // 2, fields, cells), in_specs=[VMEM] * 2, out_specs=VMEM, compiler_params=PARAMS,
        name="join",
    )(sums, got)
    groups = [[i * cols + j for i in range(rows) for j in range(side, cols, 2)] for side in range(2)]
    parts = lax.all_to_all(joined, ("mx", "my"), 0, 0, tiled=True, axis_index_groups=groups)
    tiles = pl.pallas_call(
        end_kernel, out_shape=like(1, fields, cells, dtype=F32), in_specs=[VMEM], out_specs=VMEM, compiler_params=PARAMS,
        name="end",
    )(parts)
    return sample, tiles


def solution(mesh):
    in_specs = (
        P(None, ("mx", "my")),
        P(("mx", "my"), None, None, None),
        P(("mx", "my"), None),
        P(("mx", "my"), None),
        P(("mx", "my"), None, None, None),
        P(("mx", "my"), None),
    )
    out_specs = (P(None, ("mx", "my")), P(("mx", "my"), None, None))
    return jax.shard_map(shards, mesh=mesh, in_specs=in_specs, out_specs=out_specs, check_vma=False)
```

time: 97.9 us -> 67.7 us (0.69)
  starting transfers between devices: 43.2 us -> 17.5 us
  blocking collectives: 0 us -> 14.3 us
  local copies, waits for them, and re-layouts: 11.9 us -> 4.52 us
  Pallas kernels: 25.7 us -> 19.9 us
  waiting for transfers between devices: 15.6 us -> 10.5 us
    ppermute x21 -> x17, starting transfers between devices: 43.2 us -> 17.5 us  [swap(): return lax.ppermute(block, ('mx', 'my'), route)]
    all_to_all x0 -> x1, blocking collectives: none -> 14.3 us  [shards(): lax.all_to_all(joined, ('mx', 'my'), 0, 0, tiled=True, axis_index_groups=...]
    unnamed x28 -> x16, local copies, waits for them, and re-layouts: 11.8 us -> 4.52 us
    ppermute x21 -> x17, waiting for transfers between devices: 15.6 us -> 10.5 us  [swap(): return lax.ppermute(block, ('mx', 'my'), route)]
    pallas_call x3, Pallas kernels: 14.4 us -> 9.71 us  [shards(): pl.pallas_call(functools.partial(step_kernel, degree), out_shape=[extende...]
    pallas_call x1, Pallas kernels: 8.13 us -> 6.99 us  [shards(): pl.pallas_call(last_kernel, out_shape=[extended, like(fields, nodes), lik...]
  transfers between devices with their start and end apart: 21 -> 17, of which waited for: 8 -> 6; matrix products, arithmetic and copies ran while one was open for 0% -> 0% of each run, Pallas kernels for 2% -> 2%
where the time goes in v2:
time: 67.7 us; the launch traced here: 67.4 us
  Pallas kernels  19.9 us (29%)
  starting transfers between devices  17.5 us (26%)
  blocking collectives  14.3 us (21%)
  waiting for transfers between devices  10.5 us (16%)
  local copies, waits for them, and re-layouts  4.52 us (7%)
  between operations  0.78 us (1%)
    ppermute x17, starting transfers between devices, swap(): return lax.ppermute(block, ('mx', 'my'), route)  17.5 us
    all_to_all x1, blocking collectives, shards(): lax.all_to_all(joined, ('mx', 'my'), 0, 0, tiled=True, axis_index_groups=...  14.3 us
    ppermute x17, waiting for transfers between devices, swap(): return lax.ppermute(block, ('mx', 'my'), route)  10.5 us
    pallas_call x3, Pallas kernels, shards(): pl.pallas_call(functools.partial(step_kernel, degree), out_shape=[extende...  9.71 us
    pallas_call x1, Pallas kernels, shards(): pl.pallas_call(last_kernel, out_shape=[extended, like(fields, nodes), lik...  6.99 us
    unnamed x16, local copies, waits for them, and re-layouts  4.52 us
    pallas_call x1, Pallas kernels, shards(): pl.pallas_call(weights_kernel, grid=(count // chunk,), out_shape=like(pai...  1.55 us
  transfers between devices with their start and end apart: 17, of which 6 were waited for; matrix products, arithmetic and copies ran while one was open for 0% of the time, Pallas kernels for 2%

profile of v2, /device:TPU:0, one launch (start us, length us, event | category | flops | bytes accessed | tf_op | source)
XLA Modules:
  0.0 67.4 jit_solution(8764030366202168576)
XLA Ops:
  0.6 0.0 copy-start.1
  0.6 1.0 %copy-done.1 = bf16[64,4096]{1,0:T(8,128)(2,1)S(1)} copy-done((bf16[64,4096]{1,0:T(8,128)(2,1)S(1)}, bf16[64,4096]{1,0:T(8,128)(2,1)}, u32[]{:S(2)}) %copy-start.1) | copy-done | bytes 524312
  1.7 0.7 %copy-done.5 = s32[4,16]{1,0:T(4,128)S(1)} copy-done((s32[4,16]{1,0:T(4,128)S(1)}, s32[4,16]{1,0:T(4,128)}, u32[]{:S(2)}) %copy-start.5) | copy-done | bytes 280
  2.4 0.9 %first.1 = (bf16[128,64,128]{2,1,0:T(8,128)(2,1)S(1)}, bf16[8,64,128]{2,1,0:T(8,128)(2,1)S(1)}, bf16[8,64,128]{2,1,0:T(8,128)(2,1)S(1)}, bf16[8,64,128]{2,1,0:T(8,128)(2,1)S(1)}, bf16[8,64,128]{2,1,0:T(8,128)(2,1)S(1)}) custom-call(s32[4,16]{1,0:T(4,128)S(1)} %copy-done.5, bf16[64,4096]{1,0:T(8,128)(2,1)S(1)} %copy-done.1), custom_call_target="tpu_custom_call" | custom-call | tf_op jit(solution)/shard_map/first/pallas_call | solution.py:213
  3.3 3.4 %collective-permute-start = (bf16[8,64,128]{2,1,0:T(8,128)(2,1)S(1)}, bf16[8,64,128]{2,1,0:T(8,128)(2,1)S(1)}, u32[]{:S(2)}, u32[]{:S(2)}) collective-permute-start(bf16[8,64,128]{2,1,0:T(8,128)(2,1)S(1)} %get-tuple-element.30), channel_id=1, source_target_pairs={{0,7},{1,2},{2,1},{3,4},{4,3},{5,6},{6,5},{7,0},{8,15},{9,10},{10,... | collective-permute-start | bytes 393224 | tf_op jit(solution)/shard_map/ppermute | solution.py:174
  6.7 1.6 %collective-permute-start.1 = (bf16[8,64,128]{2,1,0:T(8,128)(2,1)S(1)}, bf16[8,64,128]{2,1,0:T(8,128)(2,1)S(1)}, u32[]{:S(2)}, u32[]{:S(2)}) collective-permute-start(bf16[8,64,128]{2,1,0:T(8,128)(2,1)S(1)} %get-tuple-element.31), channel_id=1, source_target_pairs={{0,8},{1,9},{2,10},{3,11},{4,12},{5,13},{6,14},{7,15},{8,0},{9,1},... | collective-permute-start | bytes 393224 | tf_op jit(solution)/shard_map/ppermute | solution.py:174
  8.3 0.0 collective-permute-start.2
  8.3 0.5 collective-permute-start.3
  8.8 2.8 %copy-done = bf16[64,6,64,64]{3,2,1,0:T(8,128)(2,1)S(1)} copy-done((bf16[64,6,64,64]{3,2,1,0:T(8,128)(2,1)S(1)}, bf16[64,6,64,64]{3,2,1,0:T(8,128)(2,1)}, u32[]{:S(2)}) %copy-start) | copy-done | bytes 3145752
  11.6 1.6 %weights.1.weights_ref = bf16[32,768,128]{2,1,0:T(8,128)(2,1)S(1)} custom-call(bf16[64,384,64]{2,1,0:T(8,128)(2,1)S(1)} %bitcast.3), custom_call_target="tpu_custom_call" | custom-call | tf_op jit(solution)/shard_map/weights/pallas_call | solution.py:219
  13.2 0.0 collective-permute-done.halo_a
  13.2 0.0 collective-permute-done.1.halo_b
  13.2 0.0 collective-permute-done.2.halo_c
  13.2 0.0 collective-permute-done.3.halo_d
  13.2 2.9 %step1.1 = (bf16[128,64,128]{2,1,0:T(8,128)(2,1)S(1)}, f32[32,64,128]{2,1,0:T(8,128)S(1)}, f32[32,64,128]{2,1,0:T(8,128)S(1)}, bf16[128,64,128]{2,1,0:T(8,128)(2...) custom-call(s32[4,16]{1,0:T(4,128)S(1)} %copy-done.6, ...), custom_call_target="tpu_custom_call", output_to_operand_aliasing={{0}: (8, {})} | custom-call | tf_op jit(solution)/shard_map/step1/pallas_call | solution.py:229
  16.2 0.5 collective-permute-start.4
  16.7 2.9 %collective-permute-start.5 = (bf16[8,64,128]{2,1,0:T(8,128)(2,1)S(1)}, bf16[8,64,128]{2,1,0:T(8,128)(2,1)S(1)}, u32[]{:S(2)}, u32[]{:S(2)}) collective-permute-start(bf16[8,64,128]{2,1,0:T(8,128)(2,1)S(1)} %get-tuple-element.36), channel_id=1, source_target_pairs={{0,8},{1,9},{2,10},{3,11},{4,12},{5,13},{6,14},{7,15},{8,0},{9,1},... | collective-permute-start | bytes 393224 | tf_op jit(solution)/shard_map/ppermute | solution.py:174
  19.6 0.0 collective-permute-start.6
  19.6 0.5 collective-permute-start.7
  20.1 2.5 %collective-permute-done.4.halo_a = bf16[8,64,128]{2,1,0:T(8,128)(2,1)S(1)} collective-permute-done((bf16[8,64,128]{2,1,0:T(8,128)(2,1)S(1)}, bf16[8,64,128]{2,1,0:T(8,128)(2,1)S(1)}, u32[]{:S(2)}, u32[]{:S(2)}) %collective-permute-start.4) | collective-permute-done | bytes 131104 | tf_op jit(solution)/shard_map/ppermute | solution.py:174
  22.6 0.7 %collective-permute-done.5.halo_b = bf16[8,64,128]{2,1,0:T(8,128)(2,1)S(1)} collective-permute-done((bf16[8,64,128]{2,1,0:T(8,128)(2,1)S(1)}, bf16[8,64,128]{2,1,0:T(8,128)(2,1)S(1)}, u32[]{:S(2)}, u32[]{:S(2)}) %collective-permute-start.5) | collective-permute-done | bytes 131104 | tf_op jit(solution)/shard_map/ppermute | solution.py:174
  23.3 0.0 collective-permute-done.6.halo_c
  23.3 0.0 collective-permute-done.7.halo_d
  23.3 2.9 %step2.1 = (bf16[128,64,128]{2,1,0:T(8,128)(2,1)S(1)}, f32[32,64,128]{2,1,0:T(8,128)S(1)}, f32[32,64,128]{2,1,0:T(8,128)S(1)}, bf16[128,64,128]{2,1,0:T(8,128)(2...) custom-call(s32[4,16]{1,0:T(4,128)S(1)} %copy-done.6, ...), custom_call_target="tpu_custom_call", output_to_operand_aliasing={{0}: (9, {})} | custom-call | tf_op jit(solution)/shard_map/step2/pallas_call | solution.py:229
  26.2 1.6 %collective-permute-start.8 = (bf16[8,64,128]{2,1,0:T(8,128)(2,1)S(1)}, bf16[8,64,128]{2,1,0:T(8,128)(2,1)S(1)}, u32[]{:S(2)}, u32[]{:S(2)}) collective-permute-start(bf16[8,64,128]{2,1,0:T(8,128)(2,1)S(1)} %get-tuple-element.41), channel_id=1, source_target_pairs={{0,7},{1,2},{2,1},{3,4},{4,3},{5,6},{6,5},{7,0},{8,15},{9,10},{10,... | collective-permute-start | bytes 393224 | tf_op jit(solution)/shard_map/ppermute | solution.py:174
  27.8 2.2 %collective-permute-start.9 = (bf16[8,64,128]{2,1,0:T(8,128)(2,1)S(1)}, bf16[8,64,128]{2,1,0:T(8,128)(2,1)S(1)}, u32[]{:S(2)}, u32[]{:S(2)}) collective-permute-start(bf16[8,64,128]{2,1,0:T(8,128)(2,1)S(1)} %get-tuple-element.42), channel_id=1, source_target_pairs={{0,8},{1,9},{2,10},{3,11},{4,12},{5,13},{6,14},{7,15},{8,0},{9,1},... | collective-permute-start | bytes 393224 | tf_op jit(solution)/shard_map/ppermute | solution.py:174
  30.0 0.0 collective-permute-start.10
  30.0 0.5 collective-permute-start.11
  30.5 1.9 %collective-permute-done.8.halo_a = bf16[8,64,128]{2,1,0:T(8,128)(2,1)S(1)} collective-permute-done((bf16[8,64,128]{2,1,0:T(8,128)(2,1)S(1)}, bf16[8,64,128]{2,1,0:T(8,128)(2,1)S(1)}, u32[]{:S(2)}, u32[]{:S(2)}) %collective-permute-start.8) | collective-permute-done | bytes 131104 | tf_op jit(solution)/shard_map/ppermute | solution.py:174
  32.4 0.9 %collective-permute-done.9.halo_b = bf16[8,64,128]{2,1,0:T(8,128)(2,1)S(1)} collective-permute-done((bf16[8,64,128]{2,1,0:T(8,128)(2,1)S(1)}, bf16[8,64,128]{2,1,0:T(8,128)(2,1)S(1)}, u32[]{:S(2)}, u32[]{:S(2)}) %collective-permute-start.9) | collective-permute-done | bytes 131104 | tf_op jit(solution)/shard_map/ppermute | solution.py:174
  33.3 0.0 collective-permute-done.10.halo_c
  33.3 0.0 collective-permute-done.11.halo_d
  33.3 0.0 copy-start.7
  33.3 3.9 %step3.1 = (bf16[128,64,128]{2,1,0:T(8,128)(2,1)S(1)}, f32[32,64,128]{2,1,0:T(8,128)}, f32[32,64,128]{2,1,0:T(8,128)S(1)}, bf16[128,64,128]{2,1,0:T(8,128)(2,1)S...) custom-call(s32[4,16]{1,0:T(4,128)S(1)} %copy-done.6, ...), custom_call_target="tpu_custom_call", output_to_operand_aliasing={{0}: (9, {})} | custom-call | tf_op jit(solution)/shard_map/step3/pallas_call | solution.py:229
  37.2 0.9 %collective-permute-start.12 = (bf16[8,64,128]{2,1,0:T(8,128)(2,1)S(1)}, bf16[8,64,128]{2,1,0:T(8,128)(2,1)S(1)}, u32[]{:S(2)}, u32[]{:S(2)}) collective-permute-start(bf16[8,64,128]{2,1,0:T(8,128)(2,1)S(1)} %get-tuple-element.48), channel_id=1, source_target_pairs={{0,7},{1,2},{2,1},{3,4},{4,3},{5,6},{6,5},{7,0},{8,15},{9,10},{10,... | collective-permute-start | bytes 393224 | tf_op jit(solution)/shard_map/ppermute | solution.py:174
  38.1 2.3 %collective-permute-start.13 = (bf16[8,64,128]{2,1,0:T(8,128)(2,1)S(1)}, bf16[8,64,128]{2,1,0:T(8,128)(2,1)S(1)}, u32[]{:S(2)}, u32[]{:S(2)}) collective-permute-start(bf16[8,64,128]{2,1,0:T(8,128)(2,1)S(1)} %get-tuple-element.49), channel_id=1, source_target_pairs={{0,8},{1,9},{2,10},{3,11},{4,12},{5,13},{6,14},{7,15},{8,0},{9,1},... | collective-permute-start | bytes 393224 | tf_op jit(solution)/shard_map/ppermute | solution.py:174
  40.4 0.0 collective-permute-start.14
  40.4 0.5 collective-permute-start.15
  40.9 2.9 %collective-permute-done.12.halo_a = bf16[8,64,128]{2,1,0:T(8,128)(2,1)S(1)} collective-permute-done((bf16[8,64,128]{2,1,0:T(8,128)(2,1)S(1)}, bf16[8,64,128]{2,1,0:T(8,128)(2,1)S(1)}, u32[]{:S(2)}, u32[]{:S(2)}) %collective-permute-start.12) | collective-permute-done | bytes 131104 | tf_op jit(solution)/shard_map/ppermute | solution.py:174
  43.8 0.0 collective-permute-done.13.halo_b
  43.8 0.0 collective-permute-done.14.halo_c
  43.8 0.0 collective-permute-done.15.halo_d
  43.9 7.0 %last.1 = (bf16[128,64,128]{2,1,0:T(8,128)(2,1)S(1)}, bf16[64,4096]{1,0:T(8,128)(2,1)}, f32[32,64,128]{2,1,0:T(8,128)S(1)}, bf16[16,64,128]{2,1,0:T(8,128)(2,1)S(1)}) custom-call(s32[6,64]{1,0:T(8,128)S(1)} %bitcast.7, s32[2,64]{1,0:T(2,128)S(1)} %bitcast.8, bf16[32,768,128]{2,1,0:T(8,128)(2,1)S(1)} %weights.1.weights_ref, ...), custom_call_target="tpu_custom_call", output_to_operand_aliasing={{0}: (10, {})} | custom-call | tf_op jit(solution)/shard_map/last/pallas_call | solution.py:237
  50.9 0.0 collective-permute-start.16
  50.9 1.5 %collective-permute-done.16.got_ref = bf16[16,64,128]{2,1,0:T(8,128)(2,1)S(1)} collective-permute-done((bf16[16,64,128]{2,1,0:T(8,128)(2,1)S(1)}, bf16[16,64,128]{2,1,0:T(8,128)(2,1)S(1)}, u32[]{:S(2)}, u32[]{:S(2)}) %collective-permute-start.16) | collective-permute-done | bytes 262176 | tf_op jit(solution)/shard_map/ppermute | solution.py:174
  52.4 0.1 join.1
  52.5 14.3 %all_to_all.5.parts_ref = bf16[16,64,128]{2,1,0:T(8,128)(2,1)S(1)} all-to-all(bf16[16,64,128]{2,1,0:T(8,128)(2,1)S(1)} %join.1), channel_id=1, replica_groups={{0,2,4,6,8,10,12,14,16,18,20,22,24,26,28,30},{1,3,5,7,9,11,13,15,17,19,..., dimensions={0} | all-to-all | bytes 524288 | tf_op jit(solution)/shard_map/all_to_all | solution.py:249
  66.8 0.7 end.1
  (11 shorter events, 0.0 us)
Async XLA Ops:
  0.6 1.0 %copy-start.1 = (bf16[64,4096]{1,0:T(8,128)(2,1)S(1)}, bf16[64,4096]{1,0:T(8,128)(2,1)}, u32[]{:S(2)}) copy-start(bf16[64,4096]{1,0:T(8,128)(2,1)} %rest_0_.3) | copy-start | bytes 1572868
  1.7 0.7 %copy-start.5 = (s32[4,16]{1,0:T(4,128)S(1)}, s32[4,16]{1,0:T(4,128)}, u32[]{:S(2)}) copy-start(s32[4,16]{1,0:T(4,128)} %sends_ref.7) | copy-start | bytes 772
  3.3 9.9 %collective-permute-start = (bf16[8,64,128]{2,1,0:T(8,128)(2,1)S(1)}, bf16[8,64,128]{2,1,0:T(8,128)(2,1)S(1)}, u32[]{:S(2)}, u32[]{:S(2)}) collective-permute-start(bf16[8,64,128]{2,1,0:T(8,128)(2,1)S(1)} %get-tuple-element.30), channel_id=1, source_target_pairs={{0,7},{1,2},{2,1},{3,4},{4,3},{5,6},{6,5},{7,0},{8,15},{9,10},{10,... | collective-permute-start | bytes 393224 | tf_op jit(solution)/shard_map/ppermute | solution.py:174
  6.7 6.5 %collective-permute-start.1 = (bf16[8,64,128]{2,1,0:T(8,128)(2,1)S(1)}, bf16[8,64,128]{2,1,0:T(8,128)(2,1)S(1)}, u32[]{:S(2)}, u32[]{:S(2)}) collective-permute-start(bf16[8,64,128]{2,1,0:T(8,128)(2,1)S(1)} %get-tuple-element.31), channel_id=1, source_target_pairs={{0,8},{1,9},{2,10},{3,11},{4,12},{5,13},{6,14},{7,15},{8,0},{9,1},... | collective-permute-start | bytes 393224 | tf_op jit(solution)/shard_map/ppermute | solution.py:174
  8.3 4.9 %collective-permute-start.2 = (bf16[8,64,128]{2,1,0:T(8,128)(2,1)S(1)}, bf16[8,64,128]{2,1,0:T(8,128)(2,1)S(1)}, u32[]{:S(2)}, u32[]{:S(2)}) collective-permute-start(bf16[8,64,128]{2,1,0:T(8,128)(2,1)S(1)} %get-tuple-element.32), channel_id=1, source_target_pairs={{0,1},{1,0},{2,3},{3,2},{4,5},{5,4},{6,7},{7,6},{8,16},{9,17},{10,... | collective-permute-start | bytes 393224 | tf_op jit(solution)/shard_map/ppermute | solution.py:174
  8.3 4.9 %collective-permute-start.3 = (bf16[8,64,128]{2,1,0:T(8,128)(2,1)S(1)}, bf16[8,64,128]{2,1,0:T(8,128)(2,1)S(1)}, u32[]{:S(2)}, u32[]{:S(2)}) collective-permute-start(bf16[8,64,128]{2,1,0:T(8,128)(2,1)S(1)} %get-tuple-element.33), channel_id=1, source_target_pairs={{0,1},{1,0},{2,3},{3,2},{4,5},{5,4},{6,7},{7,6},{8,9},{9,8},{10,11... | collective-permute-start | bytes 393224 | tf_op jit(solution)/shard_map/ppermute | solution.py:174
  8.8 2.8 %copy-start = (bf16[64,6,64,64]{3,2,1,0:T(8,128)(2,1)S(1)}, bf16[64,6,64,64]{3,2,1,0:T(8,128)(2,1)}, u32[]{:S(2)}) copy-start(bf16[64,6,64,64]{3,2,1,0:T(8,128)(2,1)} %param.7) | copy-start | bytes 9437188
  11.6 1.6 %copy-start.2 = (bf16[64,4096]{1,0:T(8,128)(2,1)S(1)}, bf16[64,4096]{1,0:T(8,128)(2,1)}, u32[]{:S(2)}) copy-start(bf16[64,4096]{1,0:T(8,128)(2,1)} %rest_0_.3) | copy-start | bytes 1572868
  11.6 1.6 %copy-start.4 = (s32[64,6]{0,1:T(8,128)S(1)}, s32[64,6]{0,1:T(8,128)}, u32[]{:S(2)}) copy-start(s32[64,6]{0,1:T(8,128)} %param.8) | copy-start | bytes 4612
  11.6 1.6 %copy-start.6 = (s32[4,16]{1,0:T(4,128)S(1)}, s32[4,16]{1,0:T(4,128)}, u32[]{:S(2)}) copy-start(s32[4,16]{1,0:T(4,128)} %sends_ref.7) | copy-start | bytes 772
  16.2 6.4 %collective-permute-start.4 = (bf16[8,64,128]{2,1,0:T(8,128)(2,1)S(1)}, bf16[8,64,128]{2,1,0:T(8,128)(2,1)S(1)}, u32[]{:S(2)}, u32[]{:S(2)}) collective-permute-start(bf16[8,64,128]{2,1,0:T(8,128)(2,1)S(1)} %get-tuple-element.35), channel_id=1, source_target_pairs={{0,7},{1,2},{2,1},{3,4},{4,3},{5,6},{6,5},{7,0},{8,15},{9,10},{10,... | collective-permute-start | bytes 393224 | tf_op jit(solution)/shard_map/ppermute | solution.py:174
  16.7 6.6 %collective-permute-start.5 = (bf16[8,64,128]{2,1,0:T(8,128)(2,1)S(1)}, bf16[8,64,128]{2,1,0:T(8,128)(2,1)S(1)}, u32[]{:S(2)}, u32[]{:S(2)}) collective-permute-start(bf16[8,64,128]{2,1,0:T(8,128)(2,1)S(1)} %get-tuple-element.36), channel_id=1, source_target_pairs={{0,8},{1,9},{2,10},{3,11},{4,12},{5,13},{6,14},{7,15},{8,0},{9,1},... | collective-permute-start | bytes 393224 | tf_op jit(solution)/shard_map/ppermute | solution.py:174
  19.6 3.7 %collective-permute-start.6 = (bf16[8,64,128]{2,1,0:T(8,128)(2,1)S(1)}, bf16[8,64,128]{2,1,0:T(8,128)(2,1)S(1)}, u32[]{:S(2)}, u32[]{:S(2)}) collective-permute-start(bf16[8,64,128]{2,1,0:T(8,128)(2,1)S(1)} %get-tuple-element.37), channel_id=1, source_target_pairs={{0,1},{1,0},{2,3},{3,2},{4,5},{5,4},{6,7},{7,6},{8,16},{9,17},{10,... | collective-permute-start | bytes 393224 | tf_op jit(solution)/shard_map/ppermute | solution.py:174
  19.6 3.7 %collective-permute-start.7 = (bf16[8,64,128]{2,1,0:T(8,128)(2,1)S(1)}, bf16[8,64,128]{2,1,0:T(8,128)(2,1)S(1)}, u32[]{:S(2)}, u32[]{:S(2)}) collective-permute-start(bf16[8,64,128]{2,1,0:T(8,128)(2,1)S(1)} %get-tuple-element.38), channel_id=1, source_target_pairs={{0,1},{1,0},{2,3},{3,2},{4,5},{5,4},{6,7},{7,6},{8,9},{9,8},{10,11... | collective-permute-start | bytes 393224 | tf_op jit(solution)/shard_map/ppermute | solution.py:174
  26.2 6.2 %collective-permute-start.8 = (bf16[8,64,128]{2,1,0:T(8,128)(2,1)S(1)}, bf16[8,64,128]{2,1,0:T(8,128)(2,1)S(1)}, u32[]{:S(2)}, u32[]{:S(2)}) collective-permute-start(bf16[8,64,128]{2,1,0:T(8,128)(2,1)S(1)} %get-tuple-element.41), channel_id=1, source_target_pairs={{0,7},{1,2},{2,1},{3,4},{4,3},{5,6},{6,5},{7,0},{8,15},{9,10},{10,... | collective-permute-start | bytes 393224 | tf_op jit(solution)/shard_map/ppermute | solution.py:174
  27.8 5.5 %collective-permute-start.9 = (bf16[8,64,128]{2,1,0:T(8,128)(2,1)S(1)}, bf16[8,64,128]{2,1,0:T(8,128)(2,1)S(1)}, u32[]{:S(2)}, u32[]{:S(2)}) collective-permute-start(bf16[8,64,128]{2,1,0:T(8,128)(2,1)S(1)} %get-tuple-element.42), channel_id=1, source_target_pairs={{0,8},{1,9},{2,10},{3,11},{4,12},{5,13},{6,14},{7,15},{8,0},{9,1},... | collective-permute-start | bytes 393224 | tf_op jit(solution)/shard_map/ppermute | solution.py:174
  30.0 3.3 %collective-permute-start.10 = (bf16[8,64,128]{2,1,0:T(8,128)(2,1)S(1)}, bf16[8,64,128]{2,1,0:T(8,128)(2,1)S(1)}, u32[]{:S(2)}, u32[]{:S(2)}) collective-permute-start(bf16[8,64,128]{2,1,0:T(8,128)(2,1)S(1)} %get-tuple-element.43), channel_id=1, source_target_pairs={{0,1},{1,0},{2,3},{3,2},{4,5},{5,4},{6,7},{7,6},{8,16},{9,17},{10,... | collective-permute-start | bytes 393224 | tf_op jit(solution)/shard_map/ppermute | solution.py:174
  30.0 3.3 %collective-permute-start.11 = (bf16[8,64,128]{2,1,0:T(8,128)(2,1)S(1)}, bf16[8,64,128]{2,1,0:T(8,128)(2,1)S(1)}, u32[]{:S(2)}, u32[]{:S(2)}) collective-permute-start(bf16[8,64,128]{2,1,0:T(8,128)(2,1)S(1)} %get-tuple-element.44), channel_id=1, source_target_pairs={{0,1},{1,0},{2,3},{3,2},{4,5},{5,4},{6,7},{7,6},{8,9},{9,8},{10,11... | collective-permute-start | bytes 393224 | tf_op jit(solution)/shard_map/ppermute | solution.py:174
  33.3 10.5 %copy-start.3 = (bf16[64,2,64,128]{3,2,1,0:T(8,128)(2,1)S(1)}, bf16[64,2,64,128]{3,2,1,0:T(8,128)(2,1)}, u32[]{:S(2)}) copy-start(bf16[64,2,64,128]{3,2,1,0:T(8,128)(2,1)} %proj_ref.1) | copy-start | bytes 6291460
  33.3 10.5 %copy-start.7 = (s32[64,2]{0,1:T(2,128)S(1)}, s32[64,2]{0,1:T(2,128)}, u32[]{:S(2)}) copy-start(s32[64,2]{0,1:T(2,128)} %param.11) | copy-start | bytes 1540
  37.2 6.6 %collective-permute-start.12 = (bf16[8,64,128]{2,1,0:T(8,128)(2,1)S(1)}, bf16[8,64,128]{2,1,0:T(8,128)(2,1)S(1)}, u32[]{:S(2)}, u32[]{:S(2)}) collective-permute-start(bf16[8,64,128]{2,1,0:T(8,128)(2,1)S(1)} %get-tuple-element.48), channel_id=1, source_target_pairs={{0,7},{1,2},{2,1},{3,4},{4,3},{5,6},{6,5},{7,0},{8,15},{9,10},{10,... | collective-permute-start | bytes 393224 | tf_op jit(solution)/shard_map/ppermute | solution.py:174
  38.1 5.8 %collective-permute-start.13 = (bf16[8,64,128]{2,1,0:T(8,128)(2,1)S(1)}, bf16[8,64,128]{2,1,0:T(8,128)(2,1)S(1)}, u32[]{:S(2)}, u32[]{:S(2)}) collective-permute-start(bf16[8,64,128]{2,1,0:T(8,128)(2,1)S(1)} %get-tuple-element.49), channel_id=1, source_target_pairs={{0,8},{1,9},{2,10},{3,11},{4,12},{5,13},{6,14},{7,15},{8,0},{9,1},... | collective-permute-start | bytes 393224 | tf_op jit(solution)/shard_map/ppermute | solution.py:174
  40.4 3.5 %collective-permute-start.14 = (bf16[8,64,128]{2,1,0:T(8,128)(2,1)S(1)}, bf16[8,64,128]{2,1,0:T(8,128)(2,1)S(1)}, u32[]{:S(2)}, u32[]{:S(2)}) collective-permute-start(bf16[8,64,128]{2,1,0:T(8,128)(2,1)S(1)} %get-tuple-element.50), channel_id=1, source_target_pairs={{0,1},{1,0},{2,3},{3,2},{4,5},{5,4},{6,7},{7,6},{8,16},{9,17},{10,... | collective-permute-start | bytes 393224 | tf_op jit(solution)/shard_map/ppermute | solution.py:174
  40.4 3.5 %collective-permute-start.15 = (bf16[8,64,128]{2,1,0:T(8,128)(2,1)S(1)}, bf16[8,64,128]{2,1,0:T(8,128)(2,1)S(1)}, u32[]{:S(2)}, u32[]{:S(2)}) collective-permute-start(bf16[8,64,128]{2,1,0:T(8,128)(2,1)S(1)} %get-tuple-element.51), channel_id=1, source_target_pairs={{0,1},{1,0},{2,3},{3,2},{4,5},{5,4},{6,7},{7,6},{8,9},{9,8},{10,11... | collective-permute-start | bytes 393224 | tf_op jit(solution)/shard_map/ppermute | solution.py:174
  50.9 1.5 %collective-permute-start.16 = (bf16[16,64,128]{2,1,0:T(8,128)(2,1)S(1)}, bf16[16,64,128]{2,1,0:T(8,128)(2,1)S(1)}, u32[]{:S(2)}, u32[]{:S(2)}) collective-permute-start(bf16[16,64,128]{2,1,0:T(8,128)(2,1)S(1)} %get-tuple-element.57), channel_id=1, source_target_pairs={{0,1},{1,0},{2,3},{3,2},{4,5},{5,4},{6,7},{7,6},{8,9},{9,8},{10,11... | collective-permute-start | bytes 786440 | tf_op jit(solution)/shard_map/ppermute | solution.py:174
